TPU v7x, 1024 devices: a whole 4x4x32 slice. The times are simulated.
1024 devices in a mesh: energy: 64 (over y, z_lo, core), kz: 16 (over x, z_hi).
Axes of the slice: x: 4, y: 4, z: 32 (z_hi: 4, z_lo: 8; z = z_hi * 8 + z_lo), core: 2. Of those that a mesh axis runs over, the one named last changes fastest.
Arguments:
- g_less: bfloat16 [16, 192, 1, 2, 128, 128], P('kz', 'energy'), may hold values from -6 to 6
- g_ret: bfloat16 [16, 192, 1, 1, 2, 128, 128], P('kz', 'energy'), may hold values from -0.59765625 to 0.59765625
- neighbors: int32 [1, 32, 4], replicated, may hold values from 0 to 31, as said below
- ph_shift: int32 [2], replicated, may hold values from 1 to 3, as said below
- q_table: int32 [16, 16], replicated, may hold values from 0 to 15
- coupling: float32 [2, 16], replicated, may hold values from 0.2 to 2
- occupation: float32 [2], replicated, may hold values from 0.05 to 3
Outputs:
- g_next: bfloat16 [16, 192, 1, 2, 128, 128], P('kz', 'energy')
Inputs may be any that keep to these rules, and one draw needn't show every extreme that they name: `neighbors`: each atom's 4 neighbours are distinct atoms of its slab other than itself. `ph_shift`: the modes' shifts are distinct; one of them is 3.
All inputs are finite; a program needn't handle non-finite values.
Results may differ from a plain program's by a relative error of at most 0.0057.
Values may be sent and summed in bfloat16 or wider, within the bound.
A program may use at most 32 MiB of HBM per device.

v0:
```python
import jax
import jax.numpy as jnp
from jax import lax
from jax.sharding import PartitionSpec as P

ORB = 4
NMODE = 2


def padded(cells, sides, width):
    for axis, dim in sides:
        count = lax.axis_size(axis)
        ends = count - 1
        head = lax.slice_in_dim(cells, 0, width, axis=dim)
        tail = lax.slice_in_dim(cells, cells.shape[dim] - width, cells.shape[dim], axis=dim)
        cells = jnp.concatenate(
            [
                lax.ppermute(tail, axis, [(i, (i + 1) % count) for i in range(ends)]),
                cells,
                lax.ppermute(head, axis, [((i + 1) % count, i) for i in range(ends)]),
            ],
            axis=dim,
        )
    return cells


def selection(neighbors, atoms, kind):
    own = jnp.arange(atoms, dtype=jnp.int32)[None, :, None]
    pairs = jnp.concatenate([own, neighbors], axis=2)
    return (pairs[..., None] == jnp.arange(atoms, dtype=jnp.int32)).astype(kind)


def per_device(g_less, g_ret, neighbors, ph_shift, q_table, coupling, occupation):
    edev = g_less.shape[1]
    slabs = g_less.shape[2]
    width = g_less.shape[4]
    atoms = width // ORB
    members = neighbors.shape[2] + 1
    select = selection(neighbors, atoms, jnp.bfloat16)
    blocks = g_less[0].reshape(edev, slabs, 2, atoms, ORB, atoms, ORB)
    picked = jnp.einsum("esnaobp,sajb->esnaojp", blocks, select, preferred_element_type=jnp.float32)
    picked = picked.astype(jnp.bfloat16).reshape(1, edev, slabs, -1)
    entries = picked.shape[3]
    momenta = lax.axis_size("kz")
    own_row = lax.dynamic_slice_in_dim(q_table, lax.axis_index("kz"), 1, 0)[0]
    widened = padded(picked, (("energy", 1),), edev)
    start_sum = jnp.zeros((edev, slabs, entries), jnp.float32)
    total = start_sum
    piece = lax.all_gather(widened, "kz", axis=0, tiled=True)
    onehot = (own_row[:, None] == jnp.arange(coupling.shape[1], dtype=jnp.int32)[None, :]).astype(
        jnp.float32
    )
    weights = jnp.dot(onehot, coupling.T, precision=lax.Precision.HIGHEST) / momenta
    for mode in range(NMODE):
        lower = lax.dynamic_slice_in_dim(piece, edev - ph_shift[mode], edev, 1).astype(jnp.float32)
        upper = lax.dynamic_slice_in_dim(piece, edev + ph_shift[mode], edev, 1).astype(jnp.float32)
        total = total + jnp.einsum(
            "r,resf->esf",
            weights[:, mode] * occupation[mode],
            lower,
            precision=lax.Precision.HIGHEST,
        )
        total = total + jnp.einsum(
            "r,resf->esf",
            weights[:, mode] * (occupation[mode] + 1.0),
            upper,
            precision=lax.Precision.HIGHEST,
        )
    sigma = total
    sigma = sigma.astype(jnp.bfloat16).reshape(edev, slabs, 2, atoms, ORB, members, ORB)
    dense = jnp.einsum("esnaojp,sajb->esnaobp", sigma, select, preferred_element_type=jnp.float32)
    dense = dense.astype(jnp.bfloat16).reshape(edev, slabs, 2, width, width)
    green = g_ret[0]
    green_re = green[:, :, :, 0]
    green_im = green[:, :, :, 1]
    sig_re = dense[:, :, 0]
    sig_im = dense[:, :, 1]
    prod_re = jnp.einsum("estij,etjk->estik", green_re, sig_re, preferred_element_type=jnp.float32)
    prod_re = prod_re - jnp.einsum(
        "estij,etjk->estik", green_im, sig_im, preferred_element_type=jnp.float32
    )
    prod_im = jnp.einsum("estij,etjk->estik", green_re, sig_im, preferred_element_type=jnp.float32)
    prod_im = prod_im + jnp.einsum(
        "estij,etjk->estik", green_im, sig_re, preferred_element_type=jnp.float32
    )
    prod_re = prod_re.astype(jnp.bfloat16)
    prod_im = prod_im.astype(jnp.bfloat16)
    real_part = jnp.einsum(
        "estik,estlk->esil", prod_re, green_re, preferred_element_type=jnp.float32
    )
    real_part = real_part + jnp.einsum(
        "estik,estlk->esil", prod_im, green_im, preferred_element_type=jnp.float32
    )
    imag_part = jnp.einsum(
        "estik,estlk->esil", prod_im, green_re, preferred_element_type=jnp.float32
    )
    imag_part = imag_part - jnp.einsum(
        "estik,estlk->esil", prod_re, green_im, preferred_element_type=jnp.float32
    )
    result = jnp.stack([real_part, imag_part], axis=2).astype(jnp.bfloat16)
    return result[None]


def solution(mesh):
    placed = (
        P("kz", "energy", None, None, None, None),
        P("kz", "energy", None, None, None, None, None),
        P(),
        P(),
        P(),
        P(),
        P(),
    )
    return jax.shard_map(
        per_device,
        mesh=mesh,
        in_specs=placed,
        out_specs=P("kz", "energy", None, None, None, None),
        check_vma=False,
    )
```

profile of v0, /device:TPU:24, one launch (start us, length us, event | category | flops | bytes accessed | tf_op | source)
XLA Modules:
  0.0 294.3 jit_solution(9155565709054580675)
XLA Ops:
  6.5 0.0 copy-start
  6.5 0.0 copy-start.2
  6.5 0.0 all-gather.2.cloned.1.call-start
  6.5 15.3 %reshape.166 = bf16[3,2,32,4,32,4]{5,4,3,2,1,0:T(8,128)(2,1)} reshape(bf16[1,3,1,2,128,128]{5,4,3,2,1,0:T(8,128)(2,1)} %param.7) | data formatting | bytes 393216 | tf_op jit(solution)/shard_map/reshape.6
  21.8 0.0 copy-done.2
  21.8 0.1 copy.33
  21.9 4.0 %fusion.10 = bf16[3,1,2,32,4,5,4]{5,6,4,2,0,3,1:T(4,128)(2,1)S(1)} fusion(bf16[3,2,32,4,32,4]{5,4,3,2,1,0:T(8,128)(2,1)} %reshape.166, s32[32,5]{1,0:T(8,128)S(1)} %copy.33), kind=kOutput, calls=%fused_computation.6 | convolution fusion | flops 1003520 | bytes 227968 | tf_op jit(solution)/shard_map/esnaobp,sajb->esnaojp/dot_general | solution.py:41
  25.9 0.0 copy-start.3
  25.9 0.0 copy-start.4
  25.9 0.0 copy-start.1
  25.9 0.0 copy-start.5
  25.9 4.9 %copy.35 = bf16[3,1,2,32,4,5,4]{6,5,4,3,2,0,1:T(8,128)(2,1)S(1)} copy(bf16[3,1,2,32,4,5,4]{5,6,4,2,0,3,1:T(4,128)(2,1)S(1)} %fusion.10) | data formatting | bytes 61440 | tf_op jit(solution)/shard_map/convert_element_type | solution.py:42
  30.8 1.2 reshape.167
  32.0 12.8 %collective-permute-start.1 = (bf16[1,3,1,5120]{3,1,2,0:T(4,128)(2,1)S(1)}, bf16[1,3,1,5120]{3,1,2,0:T(4,128)(2,1)S(1)}, u32[]{:S(2)}, u32[]{:S(2)}) collective-permute-start(bf16[1,3,1,5120]{3,1,2,0:T(4,128)(2,1)S(1)} %reshape.167), channel_id=1, source_target_pairs={{16,0},{32,16},{48,32},{64,48},{80,64},{96,80},{112,96},{128,112},... | collective-permute-start | bytes 92168 | tf_op jit(solution)/shard_map/ppermute | solution.py:20
  44.8 2.1 collective-permute-start
  46.9 0.0 collective-permute-done.1
  46.9 10.7 %collective-permute-done = bf16[1,3,1,5120]{3,1,2,0:T(4,128)(2,1)S(1)} collective-permute-done((bf16[1,3,1,5120]{3,1,2,0:T(4,128)(2,1)S(1)}, bf16[1,3,1,5120]{3,1,2,0:T(4,128)(2,1)S(1)}, u32[]{:S(2)}, u32[]{:S(2)}) %collective-permute-start) | collective-permute-done | bytes 30752 | tf_op jit(solution)/shard_map/ppermute | solution.py:18
  57.6 0.8 pad_maximum_fusion.1
  58.4 0.0 all-gather.2.cloned.1.call-update
  58.4 0.0 copy-done.3
  58.4 0.6 fusion.57
  63.4 0.0 copy-done.4
  63.4 0.6 fusion.56
  65.2 0.0 copy-done.1
  65.2 0.0 copy-done
  65.3 0.0 copy-done.5
  65.3 0.2 convolution_multiply_fusion
  65.5 184.3 %all-gather.2.cloned.1.call-done = bf16[16,9,1,5120]{3,1,2,0:T(8,128)(2,1)} async-done(((bf16[1,9,1,5120]{3,1,2,0:T(8,128)(2,1)}), bf16[16,9,1,5120]{3,1,2,0:T(8,128)(2,1)}) %all-gather.2.cloned.1.call-update) | async-done | bytes 1474576 | tf_op jit(solution)/shard_map/all_gather | solution.py:49
  249.7 6.2 %constant_dynamic-slice_fusion.3 = (bf16[16,3,1,5120]{3,1,2,0:T(4,128)(2,1)S(1)}, bf16[16,3,1,5120]{3,1,2,0:T(4,128)(2,1)S(1)}, bf16[16,3,1,5120]{3,1,2,0:T(4,128)(2,1)S(1)}, bf16[16,3,1,5120]{3,1,2,0:T(4,128)(2,1)S(1)}) fusion(bf16[16,9,1,5120]{3,1,2,0:T(8,128)(2,1)} %all-gather.2.cloned.1.call-done, s32[]{:T(128)S(6)} %select_n.16, s32[]{:T(128)S(6)} %select_n.18, ...), kind=kLoop, calls=%fused_computation.54 | loop fusion | bytes 3932176 | tf_op jit(solution)/shard_map/dynamic_slice | solution.py:55
  255.9 1.2 fusion.25
  257.1 1.1 fusion.27
  258.2 0.5 fusion.24
  258.7 0.5 fusion.26
  259.3 0.1 fusion.33
  259.3 0.9 reshape.172
  260.3 0.8 fusion.13
  261.1 11.4 %copy.63 = bf16[3,1,2,32,4,32,4]{4,3,6,5,0,2,1:T(8,128)(2,1)} copy(bf16[3,1,2,32,4,32,4]{5,6,4,2,0,3,1:T(4,128)(2,1)S(1)} %fusion.13) | data formatting | bytes 393216 | tf_op jit(solution)/shard_map/reshape | solution.py:72
  272.5 12.4 %reshape.189 = bf16[3,1,2,128,128]{3,4,0,2,1:T(8,128)(2,1)S(1)} reshape(bf16[3,1,2,32,4,32,4]{4,3,6,5,0,2,1:T(8,128)(2,1)} %copy.63) | data formatting | bytes 393216 | tf_op jit(solution)/shard_map/reshape | solution.py:72
  285.0 0.2 fusion.32
  285.2 0.2 fusion.31
  285.4 0.2 fusion.22
  285.6 0.2 fusion.36
  285.8 0.2 fusion.23
  286.0 0.2 fusion.37
  286.2 0.2 fusion.20
  286.5 0.2 fusion.21
  286.7 0.7 copy.49
  (5 shorter events, 0.1 us)
Async XLA Ops:
  6.5 58.7 %copy-start = (s32[16,16]{1,0:T(8,128)S(1)}, s32[16,16]{1,0:T(8,128)}, u32[]{:S(2)}) copy-start(s32[16,16]{1,0:T(8,128)} %param.11) | copy-start | bytes 3076
  6.5 15.3 %copy-start.2 = (s32[1,32,4]{1,2,0:T(4,128)S(1)}, s32[1,32,4]{1,2,0:T(4,128)}, u32[]{:S(2)}) copy-start(s32[1,32,4]{1,2,0:T(4,128)} %param.9) | copy-start | bytes 1540
  6.5 243.2 %all-gather.2.cloned.1.call-start = ((), (), s32[]{:S(2)}) async-start(), calls=%async_computation | async-start | bytes 2785280 | tf_op jit(solution)/shard_map/all_gather | solution.py:49
  25.9 32.5 %copy-start.3 = (s32[2]{0:T(128)S(1)}, s32[2]{0:T(128)}, u32[]{:S(2)}) copy-start(s32[2]{0:T(128)} %param.10) | copy-start | bytes 28
  25.9 37.5 %copy-start.4 = (f32[2]{0:T(128)S(1)}, f32[2]{0:T(128)}, u32[]{:S(2)}) copy-start(f32[2]{0:T(128)} %param.13) | copy-start | bytes 28
  25.9 39.3 %copy-start.1 = (bf16[1,3,1,1,2,128,128]{6,5,4,3,2,1,0:T(8,128)(2,1)S(1)}, bf16[1,3,1,1,2,128,128]{6,5,4,3,2,1,0:T(8,128)(2,1)}, u32[]{:S(2)}) copy-start(bf16[1,3,1,1,2,128,128]{6,5,4,3,2,1,0:T(8,128)(2,1)} %param.8) | copy-start | bytes 589828
  25.9 39.4 %copy-start.5 = (f32[2,16]{1,0:T(2,128)S(1)}, f32[2,16]{1,0:T(2,128)}, u32[]{:S(2)}) copy-start(f32[2,16]{1,0:T(2,128)} %param.12) | copy-start | bytes 388
  32.0 14.9 %collective-permute-start.1 = (bf16[1,3,1,5120]{3,1,2,0:T(4,128)(2,1)S(1)}, bf16[1,3,1,5120]{3,1,2,0:T(4,128)(2,1)S(1)}, u32[]{:S(2)}, u32[]{:S(2)}) collective-permute-start(bf16[1,3,1,5120]{3,1,2,0:T(4,128)(2,1)S(1)} %reshape.167), channel_id=1, source_target_pairs={{16,0},{32,16},{48,32},{64,48},{80,64},{96,80},{112,96},{128,112},... | collective-permute-start | bytes 92168 | tf_op jit(solution)/shard_map/ppermute | solution.py:20
  44.8 12.8 %collective-permute-start = (bf16[1,3,1,5120]{3,1,2,0:T(4,128)(2,1)S(1)}, bf16[1,3,1,5120]{3,1,2,0:T(4,128)(2,1)S(1)}, u32[]{:S(2)}, u32[]{:S(2)}) collective-permute-start(bf16[1,3,1,5120]{3,1,2,0:T(4,128)(2,1)S(1)} %reshape.167), channel_id=1, source_target_pairs={{0,16},{16,32},{32,48},{48,64},{64,80},{80,96},{96,112},{112,128},... | collective-permute-start | bytes 92168 | tf_op jit(solution)/shard_map/ppermute | solution.py:18
Sparse Core Ops, SparseCore 0:
  58.5 191.1 all-gather.1
where the time goes:
time: 295 us; the launch traced here: 294 us
  waiting for transfers between devices  195 us (66%)
  local copies, waits for them, and re-layouts  54.2 us (18%)
  between operations  19.3 us (7%)
  starting transfers between devices  14.9 us (5%)
  matrix products  10 us (3%)
    all_gather x1, waiting for transfers between devices, per_device(): piece = lax.all_gather(widened, 'kz', axis=0, tiled=True)  184 us
    reshape x2, local copies, waits for them, and re-layouts, per_device(): dense = dense.astype(jnp.bfloat16).reshape(edev, slabs, 2, width, width)  23.9 us
    another operation x2, local copies, waits for them, and re-layouts  16.2 us
    ppermute x1, starting transfers between devices, padded(): lax.ppermute(head, axis, [((i + 1) % count, i) for i in range(ends)])  12.8 us
    ppermute x1, waiting for transfers between devices, padded(): lax.ppermute(tail, axis, [(i, (i + 1) % count) for i in range(ends)])  10.7 us
    dynamic_slice x1, local copies, waits for them, and re-layouts, per_device(): lax.dynamic_slice_in_dim(piece, edev - ph_shift[mode], edev, 1)  6.16 us
  transfers between devices with their start and end apart: 3, of which 2 were waited for; matrix products, arithmetic and copies ran while one was open for 0% of the time, Pallas kernels for 0%

commit v1 on v0

v1 whole, which is shorter than its diff:
```python
import jax
import jax.numpy as jnp
from jax import lax
from jax.sharding import PartitionSpec as P

ORB = 4
NMODE = 2
ZHI = 4


def padded(cells, axis, dim, width):
    count = lax.axis_size(axis)
    ends = count - 1
    head = lax.slice_in_dim(cells, 0, width, axis=dim)
    tail = lax.slice_in_dim(cells, cells.shape[dim] - width, cells.shape[dim], axis=dim)
    return jnp.concatenate(
        [
            lax.ppermute(tail, axis, [(i, (i + 1) % count) for i in range(ends)]),
            cells,
            lax.ppermute(head, axis, [((i + 1) % count, i) for i in range(ends)]),
        ],
        axis=dim,
    )


def masks(neighbors, width):
    atoms = width // ORB
    own = jnp.arange(atoms, dtype=jnp.int32)[:, None]
    pairs = jnp.concatenate([own, neighbors[0]], axis=1)
    row_pairs = jnp.repeat(pairs, ORB, axis=0)
    col_atom = jnp.arange(width, dtype=jnp.int32) // ORB
    return (row_pairs.T[:, :, None] == col_atom[None, None, :]).astype(jnp.bfloat16)


def spread(width):
    return (jnp.arange(width)[:, None] % ORB == jnp.arange(ORB)[None, :]).astype(jnp.bfloat16)


def lookup(table, rows, cols):
    size = table.shape[0]
    r = (rows[:, None] == jnp.arange(size)[None, :]).astype(jnp.float32)
    c = (cols[:, None] == jnp.arange(size)[None, :]).astype(jnp.float32)
    t = table.astype(jnp.float32)
    return jnp.dot(jnp.dot(r, t, precision=lax.Precision.HIGHEST), c.T, precision=lax.Precision.HIGHEST)


def per_device(g_less, g_ret, neighbors, ph_shift, q_table, coupling, occupation):
    edev = g_less.shape[1]
    width = g_less.shape[4]
    members = neighbors.shape[2] + 1
    momenta = lax.axis_size("kz")
    xs = momenta // ZHI
    mask = masks(neighbors, width)
    e4 = spread(width)

    green = g_less[0, :, 0]
    held = green[:, :, None] * mask[None, None]
    picked = jnp.einsum("enjrc,cp->enjpr", held, e4, preferred_element_type=jnp.float32)
    picked = picked.astype(jnp.bfloat16).reshape(edev, 2 * members * ORB, width)

    window = padded(picked, "energy", 0, edev)
    blocks = [window]
    for d in range(1, xs):
        blocks.append(lax.ppermute(window, "kz", [(i, (i + d * ZHI) % momenta) for i in range(momenta)]))
    gathered = jnp.stack(blocks, 0)

    me = lax.axis_index("kz")
    x = me // ZHI
    h = me % ZHI
    dest = x * ZHI + (h + jnp.arange(ZHI)) % ZHI
    src = ((x - jnp.arange(xs)) % xs) * ZHI + h
    qsub = lookup(q_table, dest, src).astype(jnp.int32)
    onehot = (qsub[:, :, None] == jnp.arange(coupling.shape[1])[None, None, :]).astype(jnp.float32)
    weights = jnp.einsum("zdq,mq->mzd", onehot, coupling, precision=lax.Precision.HIGHEST) / momenta

    partial = jnp.zeros((ZHI, edev) + picked.shape[1:], jnp.float32)
    for mode in range(NMODE):
        lower = lax.dynamic_slice_in_dim(gathered, edev - ph_shift[mode], edev, 1).astype(jnp.float32)
        upper = lax.dynamic_slice_in_dim(gathered, edev + ph_shift[mode], edev, 1).astype(jnp.float32)
        partial = partial + jnp.einsum(
            "zd,derb->zerb", weights[mode] * occupation[mode], lower, precision=lax.Precision.HIGHEST
        )
        partial = partial + jnp.einsum(
            "zd,derb->zerb", weights[mode] * (occupation[mode] + 1.0), upper, precision=lax.Precision.HIGHEST
        )

    total = partial[0]
    for d in range(1, ZHI):
        pairs = [(i, (i // ZHI) * ZHI + (i % ZHI + d) % ZHI) for i in range(momenta)]
        total = total + lax.ppermute(partial[d], "kz", pairs)
    sigma = total.astype(jnp.bfloat16).reshape(edev, 2, members, ORB, width)

    tiled = jnp.einsum("enjpr,cp->enjrc", sigma, e4, preferred_element_type=jnp.float32)
    dense = jnp.sum(tiled * mask[None, None].astype(jnp.float32), axis=2).astype(jnp.bfloat16)

    greenr = g_ret[0, :, 0, 0]
    green_re = greenr[:, 0]
    green_im = greenr[:, 1]
    sig_re = dense[:, 0]
    sig_im = dense[:, 1]
    prod_re = jnp.einsum("eij,ejk->eik", green_re, sig_re, preferred_element_type=jnp.float32)
    prod_re = prod_re - jnp.einsum("eij,ejk->eik", green_im, sig_im, preferred_element_type=jnp.float32)
    prod_im = jnp.einsum("eij,ejk->eik", green_re, sig_im, preferred_element_type=jnp.float32)
    prod_im = prod_im + jnp.einsum("eij,ejk->eik", green_im, sig_re, preferred_element_type=jnp.float32)
    prod_re = prod_re.astype(jnp.bfloat16)
    prod_im = prod_im.astype(jnp.bfloat16)
    real_part = jnp.einsum("eik,elk->eil", prod_re, green_re, preferred_element_type=jnp.float32)
    real_part = real_part + jnp.einsum("eik,elk->eil", prod_im, green_im, preferred_element_type=jnp.float32)
    imag_part = jnp.einsum("eik,elk->eil", prod_im, green_re, preferred_element_type=jnp.float32)
    imag_part = imag_part - jnp.einsum("eik,elk->eil", prod_re, green_im, preferred_element_type=jnp.float32)
    result = jnp.stack([real_part, imag_part], axis=1).astype(jnp.bfloat16)
    return result[None, :, None]


def solution(mesh):
    placed = (
        P("kz", "energy", None, None, None, None),
        P("kz", "energy", None, None, None, None, None),
        P(),
        P(),
        P(),
        P(),
        P(),
    )
    return jax.shard_map(
        per_device,
        mesh=mesh,
        in_specs=placed,
        out_specs=P("kz", "energy", None, None, None, None),
        check_vma=False,
    )
```

time: 295 us -> 95 us (0.32)
  waiting for transfers between devices: 195 us -> 8.37 us
  starting transfers between devices: 14.9 us -> 68.1 us
  local copies, waits for them, and re-layouts: 54.2 us -> 3.03 us
  between operations: 19.3 us -> 6.83 us
  matrix products: 10 us -> 4.71 us
    all_gather x1 -> x0, waiting for transfers between devices: 184 us -> none  [per_device(): piece = lax.all_gather(widened, 'kz', axis=0, tiled=True)]
    ppermute x0 -> x6, starting transfers between devices: none -> 53.3 us  [the longest x3 41.9 us: per_device(): total = total + lax.ppermute(partial[d], 'kz', pairs)]
    reshape x3 -> x1, local copies, waits for them, and re-layouts: 25 us -> 0.11 us  [masks(): row_pairs = jnp.repeat(pairs, ORB, axis=0)]
    another operation x3 -> x5, local copies, waits for them, and re-layouts: 16.9 us -> 1.27 us  [the longest x1 0.69 us: per_device(): result = jnp.stack([real_part, imag_part], axis=1).astype(jnp.bfloat16)]
    ppermute x1, waiting for transfers between devices: 10.7 us -> 0.01 us  [padded(): lax.ppermute(tail, axis, [(i, (i + 1) % count) for i in range(ends)])]
    ppermute x0 -> x6, waiting for transfers between devices: none -> 8.36 us  [the longest x3 8.35 us: per_device(): total = total + lax.ppermute(partial[d], 'kz', pairs)]
    dynamic_slice x1 -> x0, local copies, waits for them, and re-layouts: 6.16 us -> none  [per_device(): lax.dynamic_slice_in_dim(piece, edev - ph_shift[mode], edev, 1)]
    dot_general x15 -> x17, matrix products: 10 us -> 4.71 us  [the longest x2 0.71 us: per_device(): jnp.einsum('zd,derb->zerb', weights[mode] * (occupation[mode] + 1.0), upp...]
  transfers between devices with their start and end apart: 3 -> 8, of which waited for: 2 -> 2; matrix products, arithmetic and copies ran while one was open for 0% -> 4% of each run, Pallas kernels for 0% -> 0%
where the time goes in v1:
time: 95 us; the launch traced here: 94.2 us
  starting transfers between devices  68.1 us (72%)
  waiting for transfers between devices  8.37 us (9%)
  between operations  6.83 us (7%)
  matrix products  4.71 us (5%)
  other arithmetic  3.2 us (3%)
  local copies, waits for them, and re-layouts  3.03 us (3%)
    ppermute x3, starting transfers between devices, per_device(): total = total + lax.ppermute(partial[d], 'kz', pairs)  41.9 us
    ppermute x1, starting transfers between devices, padded(): lax.ppermute(head, axis, [((i + 1) % count, i) for i in range(ends)])  12.8 us
    ppermute x3, starting transfers between devices, per_device(): lax.ppermute(window, 'kz', [(i, (i + d * ZHI) % momenta) for i in range(m...  11.4 us
    ppermute x3, waiting for transfers between devices, per_device(): total = total + lax.ppermute(partial[d], 'kz', pairs)  8.35 us
    ppermute x1, starting transfers between devices, padded(): lax.ppermute(tail, axis, [(i, (i + 1) % count) for i in range(ends)])  2.06 us
  transfers between devices with their start and end apart: 8, of which 2 were waited for; matrix products, arithmetic and copies ran while one was open for 4% of the time, Pallas kernels for 0%

profile of v1, /device:TPU:24, one launch (start us, length us, event | category | flops | bytes accessed | tf_op | source)
XLA Modules:
  0.0 94.2 jit_solution(3497160786993942183)
XLA Ops:
  0.0 0.7 pad_add_fusion
  0.8 0.1 broadcast_in_dim.2
  0.9 0.1 reshape.135
  1.0 0.2 fusion.19
  1.1 0.0 copy-start.2
  1.1 0.0 copy-start.5
  1.2 0.4 convolution_convert_fusion
  1.5 2.1 %collective-permute-start = (bf16[3,40,128]{2,1,0:T(8,128)(2,1)S(1)}, bf16[3,40,128]{2,1,0:T(8,128)(2,1)S(1)}, u32[]{:S(2)}, u32[]{:S(2)}) collective-permute-start(bf16[3,40,128]{2,1,0:T(8,128)(2,1)S(1)} %bitcast.117), channel_id=1, source_target_pairs={{0,16},{16,32},{32,48},{48,64},{64,80},{80,96},{96,112},{112,128},... | collective-permute-start | bytes 92168 | tf_op jit(solution)/shard_map/ppermute | solution.py:18
  3.6 12.8 %collective-permute-start.1 = (bf16[3,40,128]{2,1,0:T(8,128)(2,1)S(1)}, bf16[3,40,128]{2,1,0:T(8,128)(2,1)S(1)}, u32[]{:S(2)}, u32[]{:S(2)}) collective-permute-start(bf16[3,40,128]{2,1,0:T(8,128)(2,1)S(1)} %bitcast.118), channel_id=1, source_target_pairs={{16,0},{32,16},{48,32},{64,48},{80,64},{96,80},{112,96},{128,112},... | collective-permute-start | bytes 92168 | tf_op jit(solution)/shard_map/ppermute | solution.py:20
  16.4 0.6 fusion.43
  18.4 0.2 fusion.20
  18.6 0.2 convolution_convert_fusion.1
  18.8 0.3 fusion.6
  19.1 1.4 %slice_multiply_fusion = (f32[1,4,4]{2,0,1:T(1,128)S(1)}, f32[1,4,4]{2,0,1:T(1,128)S(1)}, f32[1,4,4]{2,0,1:T(1,128)S(1)}, f32[1,4,4]{2,0,1:T(1,128)S(1)}) fusion(f32[2,4,4]{2,0,1:T(2,128)S(1)} %fusion.6, f32[]{:T(128)S(6)} %add.160, f32[]{:T(128)S(6)} %add.151, f32[]{:T(128)} %bitcast.25, f32[]{:T(128)} %bitcast.2), kind=kLoop, calls=%fused_computation.58 | loop fusion | flops 64 | bytes 400 | tf_op jit(solution)/shard_map/mul | solution.py:84
  20.4 0.0 collective-permute-done
  20.4 0.0 collective-permute-done.1
  20.5 3.4 %collective-permute-start.2 = (bf16[9,40,128]{2,1,0:T(8,128)(2,1)S(1)}, bf16[9,40,128]{2,1,0:T(8,128)(2,1)S(1)}, u32[]{:S(2)}, u32[]{:S(2)}) collective-permute-start(bf16[9,40,128]{2,1,0:T(8,128)(2,1)S(1)} %get-tuple-element.10), channel_id=1, source_target_pairs={{0,4},{1,5},{2,6},{3,7},{4,8},{5,9},{6,10},{7,11},{8,12},{9,13},{1... | collective-permute-start | bytes 276488 | tf_op jit(solution)/shard_map/ppermute | solution.py:64
  23.9 4.6 %collective-permute-start.3 = (bf16[9,40,128]{2,1,0:T(8,128)(2,1)S(1)}, bf16[9,40,128]{2,1,0:T(8,128)(2,1)S(1)}, u32[]{:S(2)}, u32[]{:S(2)}) collective-permute-start(bf16[9,40,128]{2,1,0:T(8,128)(2,1)S(1)} %get-tuple-element.10), channel_id=1, source_target_pairs={{0,8},{1,9},{2,10},{3,11},{4,12},{5,13},{6,14},{7,15},{8,0},{9,1},... | collective-permute-start | bytes 276488 | tf_op jit(solution)/shard_map/ppermute | solution.py:64
  28.5 3.3 %collective-permute-start.4 = (bf16[9,40,128]{2,1,0:T(8,128)(2,1)S(1)}, bf16[9,40,128]{2,1,0:T(8,128)(2,1)S(1)}, u32[]{:S(2)}, u32[]{:S(2)}) collective-permute-start(bf16[9,40,128]{2,1,0:T(8,128)(2,1)S(1)} %get-tuple-element.10), channel_id=1, source_target_pairs={{0,12},{1,13},{2,14},{3,15},{4,0},{5,1},{6,2},{7,3},{8,4},{9,5},{1... | collective-permute-start | bytes 276488 | tf_op jit(solution)/shard_map/ppermute | solution.py:64
  31.9 0.6 fusion.42
  37.6 0.1 copy.69
  37.7 0.0 collective-permute-done.2
  37.7 0.1 copy.70
  37.9 0.1 copy.71
  38.1 0.1 copy.72
  38.2 0.9 pad_maximum_fusion
  39.1 0.3 fusion.13
  39.4 0.4 convolution_add_fusion.2
  39.8 0.4 convolution_add_fusion.1
  40.2 0.4 convolution_add_fusion
  40.5 0.0 copy-start.1
  40.5 0.2 fusion.41
  40.7 15.7 %collective-permute-start.5 = (f32[3,40,128]{2,1,0:T(8,128)S(1)}, f32[3,40,128]{2,1,0:T(8,128)S(1)}, u32[]{:S(2)}, u32[]{:S(2)}) collective-permute-start(f32[3,40,128]{2,1,0:T(8,128)S(1)} %bitcast.116), channel_id=1, source_target_pairs={{0,1},{1,2},{2,3},{3,0},{4,5},{5,6},{6,7},{7,4},{8,9},{9,10},{10,1... | collective-permute-start | bytes 184328 | tf_op jit(solution)/shard_map/ppermute | solution.py:90
  56.5 17.7 %collective-permute-start.6 = (f32[3,40,128]{2,1,0:T(8,128)S(1)}, f32[3,40,128]{2,1,0:T(8,128)S(1)}, u32[]{:S(2)}, u32[]{:S(2)}) collective-permute-start(f32[3,40,128]{2,1,0:T(8,128)S(1)} %bitcast.115), channel_id=1, source_target_pairs={{0,2},{1,3},{2,0},{3,1},{4,6},{5,7},{6,4},{7,5},{8,10},{9,11},{10,... | collective-permute-start | bytes 184328 | tf_op jit(solution)/shard_map/ppermute | solution.py:90
  74.2 8.4 %collective-permute-start.7 = (f32[3,40,128]{2,1,0:T(8,128)S(1)}, f32[3,40,128]{2,1,0:T(8,128)S(1)}, u32[]{:S(2)}, u32[]{:S(2)}) collective-permute-start(f32[3,40,128]{2,1,0:T(8,128)S(1)} %bitcast.114), channel_id=1, source_target_pairs={{0,3},{1,0},{2,1},{3,2},{4,7},{5,4},{6,5},{7,6},{8,11},{9,8},{10,9... | collective-permute-start | bytes 184328 | tf_op jit(solution)/shard_map/ppermute | solution.py:90
  82.7 1.3 %collective-permute-done.6 = f32[3,40,128]{2,1,0:T(8,128)S(1)} collective-permute-done((f32[3,40,128]{2,1,0:T(8,128)S(1)}, f32[3,40,128]{2,1,0:T(8,128)S(1)}, u32[]{:S(2)}, u32[]{:S(2)}) %collective-permute-start.6) | collective-permute-done | bytes 61472 | tf_op jit(solution)/shard_map/ppermute | solution.py:90
  83.9 7.1 %collective-permute-done.7 = f32[3,40,128]{2,1,0:T(8,128)S(1)} collective-permute-done((f32[3,40,128]{2,1,0:T(8,128)S(1)}, f32[3,40,128]{2,1,0:T(8,128)S(1)}, u32[]{:S(2)}, u32[]{:S(2)}) %collective-permute-start.7) | collective-permute-done | bytes 61472 | tf_op jit(solution)/shard_map/ppermute | solution.py:90
  91.1 0.5 multiply_reduce_fusion
  91.6 0.2 copy.76
  91.8 0.2 fusion.15
  92.0 0.2 fusion.16
  92.2 0.2 fusion
  92.4 0.2 fusion.18
  92.6 0.2 fusion.1
  92.8 0.2 fusion.17
  93.0 0.2 fusion.5
  93.3 0.2 fusion.4
  93.6 0.7 copy.82
  (19 shorter events, 0.1 us)
Async XLA Ops:
  0.0 18.8 %copy-start = (f32[2,16]{1,0:T(2,128)S(1)}, f32[2,16]{1,0:T(2,128)}, u32[]{:S(2)}) copy-start(f32[2,16]{1,0:T(2,128)} %param.12) | copy-start | bytes 388
  0.0 1.1 %copy-start.4 = (bf16[1,3,1,2,128,128]{5,4,3,2,1,0:T(8,128)(2,1)S(1)}, bf16[1,3,1,2,128,128]{5,4,3,2,1,0:T(8,128)(2,1)}, u32[]{:S(2)}) copy-start(bf16[1,3,1,2,128,128]{5,4,3,2,1,0:T(8,128)(2,1)} %param.7) | copy-start | bytes 589828
  1.1 15.3 %copy-start.2 = (f32[2]{0:T(128)S(1)}, f32[2]{0:T(128)}, u32[]{:S(2)}) copy-start(f32[2]{0:T(128)} %param.13) | copy-start | bytes 28
  1.1 17.2 %copy-start.5 = (s32[16,16]{1,0:T(8,128)S(1)}, s32[16,16]{1,0:T(8,128)}, u32[]{:S(2)}) copy-start(s32[16,16]{1,0:T(8,128)} %param.11) | copy-start | bytes 3076
  1.5 30.4 %copy-start.3 = (s32[2]{0:T(128)S(1)}, s32[2]{0:T(128)}, u32[]{:S(2)}) copy-start(s32[2]{0:T(128)} %param.10) | copy-start | bytes 28
  1.5 18.9 %collective-permute-start = (bf16[3,40,128]{2,1,0:T(8,128)(2,1)S(1)}, bf16[3,40,128]{2,1,0:T(8,128)(2,1)S(1)}, u32[]{:S(2)}, u32[]{:S(2)}) collective-permute-start(bf16[3,40,128]{2,1,0:T(8,128)(2,1)S(1)} %bitcast.117), channel_id=1, source_target_pairs={{0,16},{16,32},{32,48},{48,64},{64,80},{80,96},{96,112},{112,128},... | collective-permute-start | bytes 92168 | tf_op jit(solution)/shard_map/ppermute | solution.py:18
  3.6 16.8 %collective-permute-start.1 = (bf16[3,40,128]{2,1,0:T(8,128)(2,1)S(1)}, bf16[3,40,128]{2,1,0:T(8,128)(2,1)S(1)}, u32[]{:S(2)}, u32[]{:S(2)}) collective-permute-start(bf16[3,40,128]{2,1,0:T(8,128)(2,1)S(1)} %bitcast.118), channel_id=1, source_target_pairs={{16,0},{32,16},{48,32},{64,48},{80,64},{96,80},{112,96},{128,112},... | collective-permute-start | bytes 92168 | tf_op jit(solution)/shard_map/ppermute | solution.py:20
  20.5 17.2 %collective-permute-start.2 = (bf16[9,40,128]{2,1,0:T(8,128)(2,1)S(1)}, bf16[9,40,128]{2,1,0:T(8,128)(2,1)S(1)}, u32[]{:S(2)}, u32[]{:S(2)}) collective-permute-start(bf16[9,40,128]{2,1,0:T(8,128)(2,1)S(1)} %get-tuple-element.10), channel_id=1, source_target_pairs={{0,4},{1,5},{2,6},{3,7},{4,8},{5,9},{6,10},{7,11},{8,12},{9,13},{1... | collective-permute-start | bytes 276488 | tf_op jit(solution)/shard_map/ppermute | solution.py:64
  23.9 14.0 %collective-permute-start.3 = (bf16[9,40,128]{2,1,0:T(8,128)(2,1)S(1)}, bf16[9,40,128]{2,1,0:T(8,128)(2,1)S(1)}, u32[]{:S(2)}, u32[]{:S(2)}) collective-permute-start(bf16[9,40,128]{2,1,0:T(8,128)(2,1)S(1)} %get-tuple-element.10), channel_id=1, source_target_pairs={{0,8},{1,9},{2,10},{3,11},{4,12},{5,13},{6,14},{7,15},{8,0},{9,1},... | collective-permute-start | bytes 276488 | tf_op jit(solution)/shard_map/ppermute | solution.py:64
  28.5 9.5 %collective-permute-start.4 = (bf16[9,40,128]{2,1,0:T(8,128)(2,1)S(1)}, bf16[9,40,128]{2,1,0:T(8,128)(2,1)S(1)}, u32[]{:S(2)}, u32[]{:S(2)}) collective-permute-start(bf16[9,40,128]{2,1,0:T(8,128)(2,1)S(1)} %get-tuple-element.10), channel_id=1, source_target_pairs={{0,12},{1,13},{2,14},{3,15},{4,0},{5,1},{6,2},{7,3},{8,4},{9,5},{1... | collective-permute-start | bytes 276488 | tf_op jit(solution)/shard_map/ppermute | solution.py:64
  40.5 42.1 %copy-start.1 = (bf16[1,3,1,1,2,128,128]{6,5,4,3,2,1,0:T(8,128)(2,1)S(1)}, bf16[1,3,1,1,2,128,128]{6,5,4,3,2,1,0:T(8,128)(2,1)}, u32[]{:S(2)}) copy-start(bf16[1,3,1,1,2,128,128]{6,5,4,3,2,1,0:T(8,128)(2,1)} %param.8) | copy-start | bytes 589828
  40.7 42.0 %collective-permute-start.5 = (f32[3,40,128]{2,1,0:T(8,128)S(1)}, f32[3,40,128]{2,1,0:T(8,128)S(1)}, u32[]{:S(2)}, u32[]{:S(2)}) collective-permute-start(f32[3,40,128]{2,1,0:T(8,128)S(1)} %bitcast.116), channel_id=1, source_target_pairs={{0,1},{1,2},{2,3},{3,0},{4,5},{5,6},{6,7},{7,4},{8,9},{9,10},{10,1... | collective-permute-start | bytes 184328 | tf_op jit(solution)/shard_map/ppermute | solution.py:90
  56.5 27.5 %collective-permute-start.6 = (f32[3,40,128]{2,1,0:T(8,128)S(1)}, f32[3,40,128]{2,1,0:T(8,128)S(1)}, u32[]{:S(2)}, u32[]{:S(2)}) collective-permute-start(f32[3,40,128]{2,1,0:T(8,128)S(1)} %bitcast.115), channel_id=1, source_target_pairs={{0,2},{1,3},{2,0},{3,1},{4,6},{5,7},{6,4},{7,5},{8,10},{9,11},{10,... | collective-permute-start | bytes 184328 | tf_op jit(solution)/shard_map/ppermute | solution.py:90
  74.2 16.8 %collective-permute-start.7 = (f32[3,40,128]{2,1,0:T(8,128)S(1)}, f32[3,40,128]{2,1,0:T(8,128)S(1)}, u32[]{:S(2)}, u32[]{:S(2)}) collective-permute-start(f32[3,40,128]{2,1,0:T(8,128)S(1)} %bitcast.114), channel_id=1, source_target_pairs={{0,3},{1,0},{2,1},{3,2},{4,7},{5,4},{6,5},{7,6},{8,11},{9,8},{10,9... | collective-permute-start | bytes 184328 | tf_op jit(solution)/shard_map/ppermute | solution.py:90

commit v2 on v1

--- a/solution.py
+++ b/solution.py
@@ -1,6 +1,8 @@
 import jax
 import jax.numpy as jnp
 from jax import lax
+from jax.experimental import pallas as pl
+from jax.experimental.pallas import tpu as pltpu
 from jax.sharding import PartitionSpec as P
 
 ORB = 4
@@ -44,6 +46,71 @@
     return jnp.dot(jnp.dot(r, t, precision=lax.Precision.HIGHEST), c.T, precision=lax.Precision.HIGHEST)
 
 
+def exchange_kernel(part_ref, out_ref, near_r, near_l, relay_r, relay_l, far_r, far_l, send, recv):
+    me = lax.axis_index("kz")
+    x = me // ZHI
+    h = me % ZHI
+    right = x * ZHI + (h + 1) % ZHI
+    left = x * ZHI + (h + ZHI - 1) % ZHI
+    mesh = pl.DeviceIdType.MESH
+    barrier = pltpu.get_barrier_semaphore()
+    for nb in (left, right):
+        pl.semaphore_signal(barrier, 1, device_id={"kz": nb}, device_id_type=mesh)
+    pl.semaphore_wait(barrier, 2)
+    half = part_ref.shape[1] // 2
+
+    def remote(src, dst, slot, to):
+        return pltpu.make_async_remote_copy(
+            src_ref=src, dst_ref=dst, send_sem=send.at[slot], recv_sem=recv.at[slot],
+            device_id={"kz": to}, device_id_type=mesh,
+        )
+
+    to_right = remote(part_ref.at[1], near_r, 0, right)
+    to_left = remote(part_ref.at[ZHI - 1], near_l, 1, left)
+    relay_right = remote(part_ref.at[2, pl.ds(0, half)], relay_r, 2, right)
+    relay_left = remote(part_ref.at[2, pl.ds(half, half)], relay_l, 3, left)
+    for c in (to_right, to_left, relay_right, relay_left):
+        c.start()
+    relay_right.wait_recv()
+    fwd_right = remote(relay_r, far_r, 4, right)
+    fwd_right.start()
+    relay_left.wait_recv()
+    fwd_left = remote(relay_l, far_l, 5, left)
+    fwd_left.start()
+    to_right.wait()
+    to_left.wait()
+    relay_right.wait_send()
+    relay_left.wait_send()
+    fwd_right.wait()
+    fwd_left.wait()
+    total = part_ref[0] + near_r[...] + near_l[...]
+    out_ref[pl.ds(0, half)] = (total[:half] + far_r[...]).astype(out_ref.dtype)
+    out_ref[pl.ds(half, half)] = (total[half:] + far_l[...]).astype(out_ref.dtype)
+
+
+def exchange(partial):
+    _, rows, lanes = partial.shape
+    half = rows // 2
+    vmem = pltpu.VMEM
+    return pl.pallas_call(
+        exchange_kernel,
+        out_shape=jax.ShapeDtypeStruct((rows, lanes), jnp.bfloat16),
+        in_specs=[pl.BlockSpec(memory_space=vmem)],
+        out_specs=pl.BlockSpec(memory_space=vmem),
+        scratch_shapes=[
+            vmem((rows, lanes), jnp.float32),
+            vmem((rows, lanes), jnp.float32),
+            vmem((half, lanes), jnp.float32),
+            vmem((half, lanes), jnp.float32),
+            vmem((half, lanes), jnp.float32),
+            vmem((half, lanes), jnp.float32),
+            pltpu.SemaphoreType.DMA((6,)),
+            pltpu.SemaphoreType.DMA((6,)),
+        ],
+        compiler_params=pltpu.CompilerParams(collective_id=0, has_side_effects=True),
+    )(partial)
+
+
 def per_device(g_less, g_ret, neighbors, ph_shift, q_table, coupling, occupation):
     edev = g_less.shape[1]
     width = g_less.shape[4]
@@ -84,11 +151,8 @@
             "zd,derb->zerb", weights[mode] * (occupation[mode] + 1.0), upper, precision=lax.Precision.HIGHEST
         )
 
-    total = partial[0]
-    for d in range(1, ZHI):
-        pairs = [(i, (i // ZHI) * ZHI + (i % ZHI + d) % ZHI) for i in range(momenta)]
-        total = total + lax.ppermute(partial[d], "kz", pairs)
-    sigma = total.astype(jnp.bfloat16).reshape(edev, 2, members, ORB, width)
+    sigma = exchange(partial.reshape(ZHI, -1, width))
+    sigma = sigma.reshape(edev, 2, members, ORB, width)
 
     tiled = jnp.einsum("enjpr,cp->enjrc", sigma, e4, preferred_element_type=jnp.float32)
     dense = jnp.sum(tiled * mask[None, None].astype(jnp.float32), axis=2).astype(jnp.bfloat16)

time: 95 us -> 88.6 us (0.933)
  the two profiles are of different devices: /device:TPU:24 before, /device:TPU:1 now
where the time goes in v2:
time: 88.6 us; the launch traced here: 88.1 us
  Pallas kernels  43.1 us (49%)
  starting transfers between devices  25.9 us (29%)
  between operations  7.02 us (8%)
  matrix products  5.45 us (6%)
  local copies, waits for them, and re-layouts  3.56 us (4%)
  other arithmetic  3.11 us (4%)
    pallas_call x1, Pallas kernels, exchange(): pl.pallas_call(exchange_kernel, out_shape=jax.ShapeDtypeStruct((rows, lan...  43.1 us
    ppermute x1, starting transfers between devices, padded(): lax.ppermute(head, axis, [((i + 1) % count, i) for i in range(ends)])  12.4 us
    ppermute x3, starting transfers between devices, per_device(): lax.ppermute(window, 'kz', [(i, (i + d * ZHI) % momenta) for i in range(m...  8.41 us
    ppermute x1, starting transfers between devices, padded(): lax.ppermute(tail, axis, [(i, (i + 1) % count) for i in range(ends)])  5.07 us
  transfers between devices with their start and end apart: 5, of which 0 were waited for; matrix products, arithmetic and copies ran while one was open for 4% of the time, Pallas kernels for 0%

profile of v2, /device:TPU:1, one launch (start us, length us, event | category | flops | bytes accessed | tf_op | source)
XLA Modules:
  0.0 88.1 jit_solution(7443021780638115063)
XLA Ops:
  0.0 0.0 copy-start
  0.0 0.7 pad_add_fusion
  0.8 0.1 broadcast_in_dim.2
  0.9 0.1 reshape.138
  1.0 0.2 fusion.19
  1.1 0.0 copy-done.4
  1.1 0.0 copy-start.2
  1.1 0.0 copy-start.5
  1.2 0.4 convolution_convert_fusion
  1.5 5.1 %collective-permute-start = (bf16[3,40,128]{2,1,0:T(8,128)(2,1)S(1)}, bf16[3,40,128]{2,1,0:T(8,128)(2,1)S(1)}, u32[]{:S(2)}, u32[]{:S(2)}) collective-permute-start(bf16[3,40,128]{2,1,0:T(8,128)(2,1)S(1)} %bitcast.105), channel_id=1, source_target_pairs={{0,16},{16,32},{32,48},{48,64},{64,80},{80,96},{96,112},{112,128},... | collective-permute-start | bytes 92168 | tf_op jit(solution)/shard_map/ppermute | solution.py:20
  6.6 12.4 %collective-permute-start.1 = (bf16[3,40,128]{2,1,0:T(8,128)(2,1)S(1)}, bf16[3,40,128]{2,1,0:T(8,128)(2,1)S(1)}, u32[]{:S(2)}, u32[]{:S(2)}) collective-permute-start(bf16[3,40,128]{2,1,0:T(8,128)(2,1)S(1)} %bitcast.106), channel_id=1, source_target_pairs={{16,0},{32,16},{48,32},{64,48},{80,64},{96,80},{112,96},{128,112},... | collective-permute-start | bytes 92168 | tf_op jit(solution)/shard_map/ppermute | solution.py:22
  19.0 0.0 copy-done.2
  19.1 0.6 fusion.42
  20.9 0.2 fusion.20
  21.1 0.2 convolution_convert_fusion.1
  21.3 0.3 fusion.6
  21.6 1.3 %slice_multiply_fusion = (f32[1,4,4]{2,0,1:T(1,128)S(1)}, f32[1,4,4]{2,0,1:T(1,128)S(1)}, f32[1,4,4]{2,0,1:T(1,128)S(1)}, f32[1,4,4]{2,0,1:T(1,128)S(1)}) fusion(f32[2,4,4]{2,0,1:T(2,128)S(1)} %fusion.6, f32[]{:T(128)S(6)} %add.151, f32[]{:T(128)S(6)} %add.142, f32[]{:T(128)} %bitcast.25, f32[]{:T(128)} %bitcast.2), kind=kLoop, calls=%fused_computation.57 | loop fusion | flops 64 | bytes 400 | tf_op jit(solution)/shard_map/mul | solution.py:151
  22.9 0.0 collective-permute-done
  22.9 0.0 collective-permute-done.1
  23.0 1.9 %collective-permute-start.2 = (bf16[9,40,128]{2,1,0:T(8,128)(2,1)S(1)}, bf16[9,40,128]{2,1,0:T(8,128)(2,1)S(1)}, u32[]{:S(2)}, u32[]{:S(2)}) collective-permute-start(bf16[9,40,128]{2,1,0:T(8,128)(2,1)S(1)} %get-tuple-element.6), channel_id=1, source_target_pairs={{0,4},{1,5},{2,6},{3,7},{4,8},{5,9},{6,10},{7,11},{8,12},{9,13},{1... | collective-permute-start | bytes 276488 | tf_op jit(solution)/shard_map/ppermute | solution.py:131
  24.9 1.9 %collective-permute-start.3 = (bf16[9,40,128]{2,1,0:T(8,128)(2,1)S(1)}, bf16[9,40,128]{2,1,0:T(8,128)(2,1)S(1)}, u32[]{:S(2)}, u32[]{:S(2)}) collective-permute-start(bf16[9,40,128]{2,1,0:T(8,128)(2,1)S(1)} %get-tuple-element.6), channel_id=1, source_target_pairs={{0,8},{1,9},{2,10},{3,11},{4,12},{5,13},{6,14},{7,15},{8,0},{9,1},... | collective-permute-start | bytes 276488 | tf_op jit(solution)/shard_map/ppermute | solution.py:131
  26.8 4.6 %collective-permute-start.4 = (bf16[9,40,128]{2,1,0:T(8,128)(2,1)S(1)}, bf16[9,40,128]{2,1,0:T(8,128)(2,1)S(1)}, u32[]{:S(2)}, u32[]{:S(2)}) collective-permute-start(bf16[9,40,128]{2,1,0:T(8,128)(2,1)S(1)} %get-tuple-element.6), channel_id=1, source_target_pairs={{0,12},{1,13},{2,14},{3,15},{4,0},{5,1},{6,2},{7,3},{8,4},{9,5},{1... | collective-permute-start | bytes 276488 | tf_op jit(solution)/shard_map/ppermute | solution.py:131
  31.4 0.6 fusion.41
  37.4 0.1 copy.59
  37.6 0.0 collective-permute-done.2
  37.6 0.1 copy.60
  37.8 0.0 collective-permute-done.3
  37.8 0.1 copy.61
  37.9 0.0 collective-permute-done.4
  37.9 0.1 copy.62
  38.1 0.9 pad_maximum_fusion
  38.9 0.3 fusion.13
  39.3 0.4 convolution_add_fusion.2
  39.7 0.4 convolution_add_fusion.1
  40.0 0.4 convolution_add_fusion
  40.4 0.7 copy.63
  41.1 43.1 %shard_map.73 = bf16[120,128]{1,0:T(8,128)(2,1)} custom-call(f32[4,120,128]{2,1,0:T(8,128)} %bitcast.101), custom_call_target="tpu_custom_call" | custom-call | tf_op jit(solution)/shard_map/pallas_call | solution.py:95
  84.2 1.3 %multiply_reduce_fusion = bf16[3,2,128,128]{3,2,1,0:T(8,128)(2,1)S(1)} fusion(bf16[3,2,5,4,128]{4,3,2,1,0:T(4,128)(2,1)} %bitcast.108, f32[5,128,128]{2,1,0:T(8,128)S(1)} %get-tuple-element.7, s32[128]{0:T(128)S(1)} %get-tuple-element.18), kind=kOutput, calls=%fused_computation | convolution fusion | flops 4817408 | bytes 555520 | tf_op jit(solution)/shard_map/enjpr,cp->enjrc/dot_general | solution.py:157
  85.5 0.2 copy.64
  85.6 0.2 fusion.15
  85.8 0.2 fusion.16
  86.0 0.2 fusion
  86.3 0.2 fusion.18
  86.5 0.2 fusion.1
  86.7 0.2 fusion.17
  86.9 0.2 fusion.5
  87.2 0.2 fusion.4
  87.4 0.7 copy.70
  (13 shorter events, 0.1 us)
Async XLA Ops:
  0.0 21.3 %copy-start = (f32[2,16]{1,0:T(2,128)S(1)}, f32[2,16]{1,0:T(2,128)}, u32[]{:S(2)}) copy-start(f32[2,16]{1,0:T(2,128)} %param.12) | copy-start | bytes 388
  0.0 1.1 %copy-start.4 = (bf16[1,3,1,2,128,128]{5,4,3,2,1,0:T(8,128)(2,1)S(1)}, bf16[1,3,1,2,128,128]{5,4,3,2,1,0:T(8,128)(2,1)}, u32[]{:S(2)}) copy-start(bf16[1,3,1,2,128,128]{5,4,3,2,1,0:T(8,128)(2,1)} %param.7) | copy-start | bytes 589828
  1.1 17.9 %copy-start.2 = (f32[2]{0:T(128)S(1)}, f32[2]{0:T(128)}, u32[]{:S(2)}) copy-start(f32[2]{0:T(128)} %param.13) | copy-start | bytes 28
  1.1 19.8 %copy-start.5 = (s32[16,16]{1,0:T(8,128)S(1)}, s32[16,16]{1,0:T(8,128)}, u32[]{:S(2)}) copy-start(s32[16,16]{1,0:T(8,128)} %param.11) | copy-start | bytes 3076
  1.5 29.9 %copy-start.3 = (s32[2]{0:T(128)S(1)}, s32[2]{0:T(128)}, u32[]{:S(2)}) copy-start(s32[2]{0:T(128)} %param.10) | copy-start | bytes 28
  1.5 35.9 %copy-start.1 = (bf16[1,3,1,1,2,128,128]{6,5,4,3,2,1,0:T(8,128)(2,1)S(1)}, bf16[1,3,1,1,2,128,128]{6,5,4,3,2,1,0:T(8,128)(2,1)}, u32[]{:S(2)}) copy-start(bf16[1,3,1,1,2,128,128]{6,5,4,3,2,1,0:T(8,128)(2,1)} %param.8) | copy-start | bytes 589828
  1.5 21.4 %collective-permute-start = (bf16[3,40,128]{2,1,0:T(8,128)(2,1)S(1)}, bf16[3,40,128]{2,1,0:T(8,128)(2,1)S(1)}, u32[]{:S(2)}, u32[]{:S(2)}) collective-permute-start(bf16[3,40,128]{2,1,0:T(8,128)(2,1)S(1)} %bitcast.105), channel_id=1, source_target_pairs={{0,16},{16,32},{32,48},{48,64},{64,80},{80,96},{96,112},{112,128},... | collective-permute-start | bytes 92168 | tf_op jit(solution)/shard_map/ppermute | solution.py:20
  6.6 16.3 %collective-permute-start.1 = (bf16[3,40,128]{2,1,0:T(8,128)(2,1)S(1)}, bf16[3,40,128]{2,1,0:T(8,128)(2,1)S(1)}, u32[]{:S(2)}, u32[]{:S(2)}) collective-permute-start(bf16[3,40,128]{2,1,0:T(8,128)(2,1)S(1)} %bitcast.106), channel_id=1, source_target_pairs={{16,0},{32,16},{48,32},{64,48},{80,64},{96,80},{112,96},{128,112},... | collective-permute-start | bytes 92168 | tf_op jit(solution)/shard_map/ppermute | solution.py:22
  23.0 14.6 %collective-permute-start.2 = (bf16[9,40,128]{2,1,0:T(8,128)(2,1)S(1)}, bf16[9,40,128]{2,1,0:T(8,128)(2,1)S(1)}, u32[]{:S(2)}, u32[]{:S(2)}) collective-permute-start(bf16[9,40,128]{2,1,0:T(8,128)(2,1)S(1)} %get-tuple-element.6), channel_id=1, source_target_pairs={{0,4},{1,5},{2,6},{3,7},{4,8},{5,9},{6,10},{7,11},{8,12},{9,13},{1... | collective-permute-start | bytes 276488 | tf_op jit(solution)/shard_map/ppermute | solution.py:131
  24.9 12.9 %collective-permute-start.3 = (bf16[9,40,128]{2,1,0:T(8,128)(2,1)S(1)}, bf16[9,40,128]{2,1,0:T(8,128)(2,1)S(1)}, u32[]{:S(2)}, u32[]{:S(2)}) collective-permute-start(bf16[9,40,128]{2,1,0:T(8,128)(2,1)S(1)} %get-tuple-element.6), channel_id=1, source_target_pairs={{0,8},{1,9},{2,10},{3,11},{4,12},{5,13},{6,14},{7,15},{8,0},{9,1},... | collective-permute-start | bytes 276488 | tf_op jit(solution)/shard_map/ppermute | solution.py:131
  26.8 11.1 %collective-permute-start.4 = (bf16[9,40,128]{2,1,0:T(8,128)(2,1)S(1)}, bf16[9,40,128]{2,1,0:T(8,128)(2,1)S(1)}, u32[]{:S(2)}, u32[]{:S(2)}) collective-permute-start(bf16[9,40,128]{2,1,0:T(8,128)(2,1)S(1)} %get-tuple-element.6), channel_id=1, source_target_pairs={{0,12},{1,13},{2,14},{3,15},{4,0},{5,1},{6,2},{7,3},{8,4},{9,5},{1... | collective-permute-start | bytes 276488 | tf_op jit(solution)/shard_map/ppermute | solution.py:131

commit v3 on v2

--- a/solution.py
+++ b/solution.py
@@ -46,7 +46,7 @@
     return jnp.dot(jnp.dot(r, t, precision=lax.Precision.HIGHEST), c.T, precision=lax.Precision.HIGHEST)
 
 
-def exchange_kernel(part_ref, out_ref, near_r, near_l, relay_r, relay_l, far_r, far_l, send, recv):
+def exchange_kernel(part_ref, out_ref, relay_r, relay_l, near_r, near_l, far_r, far_l, sum_r, sum_l, send, recv):
     me = lax.axis_index("kz")
     x = me // ZHI
     h = me % ZHI
@@ -58,6 +58,8 @@
         pl.semaphore_signal(barrier, 1, device_id={"kz": nb}, device_id_type=mesh)
     pl.semaphore_wait(barrier, 2)
     half = part_ref.shape[1] // 2
+    lo = pl.ds(0, half)
+    hi = pl.ds(half, half)
 
     def remote(src, dst, slot, to):
         return pltpu.make_async_remote_copy(
@@ -65,27 +67,28 @@
             device_id={"kz": to}, device_id_type=mesh,
         )
 
-    to_right = remote(part_ref.at[1], near_r, 0, right)
-    to_left = remote(part_ref.at[ZHI - 1], near_l, 1, left)
-    relay_right = remote(part_ref.at[2, pl.ds(0, half)], relay_r, 2, right)
-    relay_left = remote(part_ref.at[2, pl.ds(half, half)], relay_l, 3, left)
-    for c in (to_right, to_left, relay_right, relay_left):
+    far_right = remote(part_ref.at[2, lo], relay_r, 0, right)
+    far_left = remote(part_ref.at[2, hi], relay_l, 1, left)
+    plain_right = remote(part_ref.at[1, hi], near_r, 2, right)
+    plain_left = remote(part_ref.at[ZHI - 1, lo], near_l, 3, left)
+    for c in (far_right, far_left, plain_right, plain_left):
         c.start()
-    relay_right.wait_recv()
-    fwd_right = remote(relay_r, far_r, 4, right)
-    fwd_right.start()
-    relay_left.wait_recv()
-    fwd_left = remote(relay_l, far_l, 5, left)
-    fwd_left.start()
-    to_right.wait()
-    to_left.wait()
-    relay_right.wait_send()
-    relay_left.wait_send()
-    fwd_right.wait()
-    fwd_left.wait()
-    total = part_ref[0] + near_r[...] + near_l[...]
-    out_ref[pl.ds(0, half)] = (total[:half] + far_r[...]).astype(out_ref.dtype)
-    out_ref[pl.ds(half, half)] = (total[half:] + far_l[...]).astype(out_ref.dtype)
+    far_right.wait_recv()
+    sum_r[...] = relay_r[...] + part_ref[1, lo]
+    merged_right = remote(sum_r, far_r, 4, right)
+    merged_right.start()
+    far_left.wait_recv()
+    sum_l[...] = relay_l[...] + part_ref[ZHI - 1, hi]
+    merged_left = remote(sum_l, far_l, 5, left)
+    merged_left.start()
+    plain_right.wait()
+    plain_left.wait()
+    far_right.wait_send()
+    far_left.wait_send()
+    merged_right.wait()
+    merged_left.wait()
+    out_ref[lo] = (part_ref[0, lo] + near_l[...] + far_r[...]).astype(out_ref.dtype)
+    out_ref[hi] = (part_ref[0, hi] + near_r[...] + far_l[...]).astype(out_ref.dtype)
 
 
 def exchange(partial):
@@ -97,16 +100,8 @@
         out_shape=jax.ShapeDtypeStruct((rows, lanes), jnp.bfloat16),
         in_specs=[pl.BlockSpec(memory_space=vmem)],
         out_specs=pl.BlockSpec(memory_space=vmem),
-        scratch_shapes=[
-            vmem((rows, lanes), jnp.float32),
-            vmem((rows, lanes), jnp.float32),
-            vmem((half, lanes), jnp.float32),
-            vmem((half, lanes), jnp.float32),
-            vmem((half, lanes), jnp.float32),
-            vmem((half, lanes), jnp.float32),
-            pltpu.SemaphoreType.DMA((6,)),
-            pltpu.SemaphoreType.DMA((6,)),
-        ],
+        scratch_shapes=[vmem((half, lanes), jnp.float32) for _ in range(8)]
+        + [pltpu.SemaphoreType.DMA((6,)), pltpu.SemaphoreType.DMA((6,))],
         compiler_params=pltpu.CompilerParams(collective_id=0, has_side_effects=True),
     )(partial)
 

time: 88.6 us -> 83.5 us (0.942)
  the two profiles are of different devices: /device:TPU:1 before, /device:TPU:24 now
where the time goes in v3:
time: 83.5 us; the launch traced here: 83 us
  Pallas kernels  37.7 us (45%)
  starting transfers between devices  26.2 us (31%)
  between operations  7.02 us (8%)
  matrix products  5.46 us (7%)
  local copies, waits for them, and re-layouts  3.56 us (4%)
  other arithmetic  3.11 us (4%)
    pallas_call x1, Pallas kernels, exchange(): pl.pallas_call(exchange_kernel, out_shape=jax.ShapeDtypeStruct((rows, lan...  37.7 us
    ppermute x1, starting transfers between devices, padded(): lax.ppermute(head, axis, [((i + 1) % count, i) for i in range(ends)])  12.8 us
    ppermute x3, starting transfers between devices, per_device(): lax.ppermute(window, 'kz', [(i, (i + d * ZHI) % momenta) for i in range(m...  11.4 us
    ppermute x1, starting transfers between devices, padded(): lax.ppermute(tail, axis, [(i, (i + 1) % count) for i in range(ends)])  2.06 us
  transfers between devices with their start and end apart: 5, of which 0 were waited for; matrix products, arithmetic and copies ran while one was open for 4% of the time, Pallas kernels for 0%

profile of v3, /device:TPU:24, one launch (start us, length us, event | category | flops | bytes accessed | tf_op | source)
XLA Modules:
  0.0 83.0 jit_solution(18339026877104737040)
XLA Ops:
  0.0 0.0 copy-start
  0.0 0.7 pad_add_fusion
  0.8 0.1 broadcast_in_dim.2
  0.9 0.1 reshape.138
  1.0 0.2 fusion.19
  1.1 0.0 copy-done.4
  1.1 0.0 copy-start.2
  1.1 0.0 copy-start.5
  1.2 0.4 convolution_convert_fusion
  1.5 2.1 %collective-permute-start = (bf16[3,40,128]{2,1,0:T(8,128)(2,1)S(1)}, bf16[3,40,128]{2,1,0:T(8,128)(2,1)S(1)}, u32[]{:S(2)}, u32[]{:S(2)}) collective-permute-start(bf16[3,40,128]{2,1,0:T(8,128)(2,1)S(1)} %bitcast.105), channel_id=1, source_target_pairs={{0,16},{16,32},{32,48},{48,64},{64,80},{80,96},{96,112},{112,128},... | collective-permute-start | bytes 92168 | tf_op jit(solution)/shard_map/ppermute | solution.py:20
  3.6 12.8 %collective-permute-start.1 = (bf16[3,40,128]{2,1,0:T(8,128)(2,1)S(1)}, bf16[3,40,128]{2,1,0:T(8,128)(2,1)S(1)}, u32[]{:S(2)}, u32[]{:S(2)}) collective-permute-start(bf16[3,40,128]{2,1,0:T(8,128)(2,1)S(1)} %bitcast.106), channel_id=1, source_target_pairs={{16,0},{32,16},{48,32},{64,48},{80,64},{96,80},{112,96},{128,112},... | collective-permute-start | bytes 92168 | tf_op jit(solution)/shard_map/ppermute | solution.py:22
  16.4 0.0 copy-done.2
  16.4 0.6 fusion.42
  18.3 0.2 fusion.20
  18.5 0.2 convolution_convert_fusion.1
  18.7 0.3 fusion.6
  19.0 1.3 %slice_multiply_fusion = (f32[1,4,4]{2,0,1:T(1,128)S(1)}, f32[1,4,4]{2,0,1:T(1,128)S(1)}, f32[1,4,4]{2,0,1:T(1,128)S(1)}, f32[1,4,4]{2,0,1:T(1,128)S(1)}) fusion(f32[2,4,4]{2,0,1:T(2,128)S(1)} %fusion.6, f32[]{:T(128)S(6)} %add.151, f32[]{:T(128)S(6)} %add.142, f32[]{:T(128)} %bitcast.25, f32[]{:T(128)} %bitcast.2), kind=kLoop, calls=%fused_computation.57 | loop fusion | flops 64 | bytes 400 | tf_op jit(solution)/shard_map/mul | solution.py:146
  20.3 0.0 collective-permute-done
  20.3 0.0 collective-permute-done.1
  20.3 3.4 %collective-permute-start.2 = (bf16[9,40,128]{2,1,0:T(8,128)(2,1)S(1)}, bf16[9,40,128]{2,1,0:T(8,128)(2,1)S(1)}, u32[]{:S(2)}, u32[]{:S(2)}) collective-permute-start(bf16[9,40,128]{2,1,0:T(8,128)(2,1)S(1)} %get-tuple-element.6), channel_id=1, source_target_pairs={{0,4},{1,5},{2,6},{3,7},{4,8},{5,9},{6,10},{7,11},{8,12},{9,13},{1... | collective-permute-start | bytes 276488 | tf_op jit(solution)/shard_map/ppermute | solution.py:126
  23.7 4.6 %collective-permute-start.3 = (bf16[9,40,128]{2,1,0:T(8,128)(2,1)S(1)}, bf16[9,40,128]{2,1,0:T(8,128)(2,1)S(1)}, u32[]{:S(2)}, u32[]{:S(2)}) collective-permute-start(bf16[9,40,128]{2,1,0:T(8,128)(2,1)S(1)} %get-tuple-element.6), channel_id=1, source_target_pairs={{0,8},{1,9},{2,10},{3,11},{4,12},{5,13},{6,14},{7,15},{8,0},{9,1},... | collective-permute-start | bytes 276488 | tf_op jit(solution)/shard_map/ppermute | solution.py:126
  28.4 3.3 %collective-permute-start.4 = (bf16[9,40,128]{2,1,0:T(8,128)(2,1)S(1)}, bf16[9,40,128]{2,1,0:T(8,128)(2,1)S(1)}, u32[]{:S(2)}, u32[]{:S(2)}) collective-permute-start(bf16[9,40,128]{2,1,0:T(8,128)(2,1)S(1)} %get-tuple-element.6), channel_id=1, source_target_pairs={{0,12},{1,13},{2,14},{3,15},{4,0},{5,1},{6,2},{7,3},{8,4},{9,5},{1... | collective-permute-start | bytes 276488 | tf_op jit(solution)/shard_map/ppermute | solution.py:126
  31.8 0.6 fusion.41
  37.8 0.1 copy.59
  37.9 0.0 collective-permute-done.2
  37.9 0.1 copy.60
  38.1 0.0 collective-permute-done.3
  38.1 0.1 copy.61
  38.2 0.0 collective-permute-done.4
  38.3 0.1 copy.62
  38.4 0.9 %pad_maximum_fusion = bf16[4,9,40,128]{3,0,2,1:T(4,128)(2,1)S(1)} fusion(bf16[1,9,40,128]{3,0,2,1:T(2,128)(2,1)S(1)} %copy.62, bf16[1,9,40,128]{3,0,2,1:T(2,128)(2,1)S(1)} %copy.61, bf16[1,9,40,128]{3,0,2,1:T(2,128)(2,1)S(1)} %copy.60, bf16[1,9,40,128]{3,0,2,1:T(2,128)(2,1)S(1)} %copy.59), kind=kLoop, calls=%fused_computation.21 | loop fusion | flops 1474560 | bytes 737280 | tf_op jit(solution)/shard_map/stack | solution.py:127
  39.3 0.3 fusion.13
  39.6 0.4 convolution_add_fusion.2
  40.0 0.4 convolution_add_fusion.1
  40.4 0.4 convolution_add_fusion
  40.7 0.7 copy.63
  41.4 37.7 %shard_map.73 = bf16[120,128]{1,0:T(8,128)(2,1)} custom-call(f32[4,120,128]{2,1,0:T(8,128)} %bitcast.101), custom_call_target="tpu_custom_call" | custom-call | tf_op jit(solution)/shard_map/pallas_call | solution.py:98
  79.1 1.3 %multiply_reduce_fusion = bf16[3,2,128,128]{3,2,1,0:T(8,128)(2,1)S(1)} fusion(bf16[3,2,5,4,128]{4,3,2,1,0:T(4,128)(2,1)} %bitcast.108, f32[5,128,128]{2,1,0:T(8,128)S(1)} %get-tuple-element.7, s32[128]{0:T(128)S(1)} %get-tuple-element.18), kind=kOutput, calls=%fused_computation | convolution fusion | flops 4817408 | bytes 555520 | tf_op jit(solution)/shard_map/enjpr,cp->enjrc/dot_general | solution.py:152
  80.4 0.2 copy.64
  80.6 0.2 fusion.15
  80.8 0.2 fusion.16
  81.0 0.2 fusion
  81.2 0.2 fusion.18
  81.4 0.2 fusion.1
  81.6 0.2 fusion.17
  81.8 0.2 fusion.5
  82.1 0.2 fusion.4
  82.4 0.7 copy.70
  (13 shorter events, 0.1 us)
Async XLA Ops:
  0.0 18.7 %copy-start = (f32[2,16]{1,0:T(2,128)S(1)}, f32[2,16]{1,0:T(2,128)}, u32[]{:S(2)}) copy-start(f32[2,16]{1,0:T(2,128)} %param.12) | copy-start | bytes 388
  0.0 1.1 %copy-start.4 = (bf16[1,3,1,2,128,128]{5,4,3,2,1,0:T(8,128)(2,1)S(1)}, bf16[1,3,1,2,128,128]{5,4,3,2,1,0:T(8,128)(2,1)}, u32[]{:S(2)}) copy-start(bf16[1,3,1,2,128,128]{5,4,3,2,1,0:T(8,128)(2,1)} %param.7) | copy-start | bytes 589828
  1.1 15.3 %copy-start.2 = (f32[2]{0:T(128)S(1)}, f32[2]{0:T(128)}, u32[]{:S(2)}) copy-start(f32[2]{0:T(128)} %param.13) | copy-start | bytes 28
  1.1 17.2 %copy-start.5 = (s32[16,16]{1,0:T(8,128)S(1)}, s32[16,16]{1,0:T(8,128)}, u32[]{:S(2)}) copy-start(s32[16,16]{1,0:T(8,128)} %param.11) | copy-start | bytes 3076
  1.5 30.2 %copy-start.3 = (s32[2]{0:T(128)S(1)}, s32[2]{0:T(128)}, u32[]{:S(2)}) copy-start(s32[2]{0:T(128)} %param.10) | copy-start | bytes 28
  1.5 36.2 %copy-start.1 = (bf16[1,3,1,1,2,128,128]{6,5,4,3,2,1,0:T(8,128)(2,1)S(1)}, bf16[1,3,1,1,2,128,128]{6,5,4,3,2,1,0:T(8,128)(2,1)}, u32[]{:S(2)}) copy-start(bf16[1,3,1,1,2,128,128]{6,5,4,3,2,1,0:T(8,128)(2,1)} %param.8) | copy-start | bytes 589828
  1.5 18.8 %collective-permute-start = (bf16[3,40,128]{2,1,0:T(8,128)(2,1)S(1)}, bf16[3,40,128]{2,1,0:T(8,128)(2,1)S(1)}, u32[]{:S(2)}, u32[]{:S(2)}) collective-permute-start(bf16[3,40,128]{2,1,0:T(8,128)(2,1)S(1)} %bitcast.105), channel_id=1, source_target_pairs={{0,16},{16,32},{32,48},{48,64},{64,80},{80,96},{96,112},{112,128},... | collective-permute-start | bytes 92168 | tf_op jit(solution)/shard_map/ppermute | solution.py:20
  3.6 16.7 %collective-permute-start.1 = (bf16[3,40,128]{2,1,0:T(8,128)(2,1)S(1)}, bf16[3,40,128]{2,1,0:T(8,128)(2,1)S(1)}, u32[]{:S(2)}, u32[]{:S(2)}) collective-permute-start(bf16[3,40,128]{2,1,0:T(8,128)(2,1)S(1)} %bitcast.106), channel_id=1, source_target_pairs={{16,0},{32,16},{48,32},{64,48},{80,64},{96,80},{112,96},{128,112},... | collective-permute-start | bytes 92168 | tf_op jit(solution)/shard_map/ppermute | solution.py:22
  20.3 17.6 %collective-permute-start.2 = (bf16[9,40,128]{2,1,0:T(8,128)(2,1)S(1)}, bf16[9,40,128]{2,1,0:T(8,128)(2,1)S(1)}, u32[]{:S(2)}, u32[]{:S(2)}) collective-permute-start(bf16[9,40,128]{2,1,0:T(8,128)(2,1)S(1)} %get-tuple-element.6), channel_id=1, source_target_pairs={{0,4},{1,5},{2,6},{3,7},{4,8},{5,9},{6,10},{7,11},{8,12},{9,13},{1... | collective-permute-start | bytes 276488 | tf_op jit(solution)/shard_map/ppermute | solution.py:126
  23.7 14.3 %collective-permute-start.3 = (bf16[9,40,128]{2,1,0:T(8,128)(2,1)S(1)}, bf16[9,40,128]{2,1,0:T(8,128)(2,1)S(1)}, u32[]{:S(2)}, u32[]{:S(2)}) collective-permute-start(bf16[9,40,128]{2,1,0:T(8,128)(2,1)S(1)} %get-tuple-element.6), channel_id=1, source_target_pairs={{0,8},{1,9},{2,10},{3,11},{4,12},{5,13},{6,14},{7,15},{8,0},{9,1},... | collective-permute-start | bytes 276488 | tf_op jit(solution)/shard_map/ppermute | solution.py:126
  28.4 9.9 %collective-permute-start.4 = (bf16[9,40,128]{2,1,0:T(8,128)(2,1)S(1)}, bf16[9,40,128]{2,1,0:T(8,128)(2,1)S(1)}, u32[]{:S(2)}, u32[]{:S(2)}) collective-permute-start(bf16[9,40,128]{2,1,0:T(8,128)(2,1)S(1)} %get-tuple-element.6), channel_id=1, source_target_pairs={{0,12},{1,13},{2,14},{3,15},{4,0},{5,1},{6,2},{7,3},{8,4},{9,5},{1... | collective-permute-start | bytes 276488 | tf_op jit(solution)/shard_map/ppermute | solution.py:126

commit v4 on v3

--- a/solution.py
+++ b/solution.py
@@ -8,21 +8,6 @@
 ORB = 4
 NMODE = 2
 ZHI = 4
-
-
-def padded(cells, axis, dim, width):
-    count = lax.axis_size(axis)
-    ends = count - 1
-    head = lax.slice_in_dim(cells, 0, width, axis=dim)
-    tail = lax.slice_in_dim(cells, cells.shape[dim] - width, cells.shape[dim], axis=dim)
-    return jnp.concatenate(
-        [
-            lax.ppermute(tail, axis, [(i, (i + 1) % count) for i in range(ends)]),
-            cells,
-            lax.ppermute(head, axis, [((i + 1) % count, i) for i in range(ends)]),
-        ],
-        axis=dim,
-    )
 
 
 def masks(neighbors, width):
@@ -106,6 +91,61 @@
     )(partial)
 
 
+def gather_kernel(own_ref, out_ref, land, send, recv):
+    kz = lax.axis_index("kz")
+    eb = lax.axis_index("energy")
+    ne = lax.axis_size("energy")
+    xs = lax.axis_size("kz") // ZHI
+    x = kz // ZHI
+    h = kz % ZHI
+    mesh = pl.DeviceIdType.MESH
+    peers = [(d, t) for d in range(xs) for t in (-1, 0, 1) if (d, t) != (0, 0)]
+
+    def where(d, t):
+        return {"kz": ((x + d) % xs) * ZHI + h, "energy": (eb + t + ne) % ne}
+
+    barrier = pltpu.get_barrier_semaphore()
+    for d, t in peers:
+        pl.semaphore_signal(barrier, 1, device_id=where(d, t), device_id_type=mesh)
+    pl.semaphore_wait(barrier, len(peers))
+    copies = []
+    for i, (d, t) in enumerate(peers):
+        c = pltpu.make_async_remote_copy(
+            src_ref=own_ref, dst_ref=land.at[d, 1 - t], send_sem=send.at[i], recv_sem=recv.at[i],
+            device_id=where(d, t), device_id_type=mesh,
+        )
+        c.start()
+        copies.append(c)
+    for c in copies:
+        c.wait()
+    zero = jnp.zeros(own_ref.shape, own_ref.dtype)
+    for d in range(xs):
+        if d == 0:
+            out_ref[0, 1] = own_ref[...]
+        else:
+            out_ref[d, 1] = land[d, 1]
+        out_ref[d, 0] = jnp.where(eb > 0, land[d, 0], zero)
+        out_ref[d, 2] = jnp.where(eb < ne - 1, land[d, 2], zero)
+
+
+def gather(own):
+    xs = lax.axis_size("kz") // ZHI
+    vmem = pltpu.VMEM
+    peers = 3 * xs - 1
+    return pl.pallas_call(
+        gather_kernel,
+        out_shape=jax.ShapeDtypeStruct((xs, 3) + own.shape, own.dtype),
+        in_specs=[pl.BlockSpec(memory_space=vmem)],
+        out_specs=pl.BlockSpec(memory_space=vmem),
+        scratch_shapes=[
+            vmem((xs, 3) + own.shape, own.dtype),
+            pltpu.SemaphoreType.DMA((peers,)),
+            pltpu.SemaphoreType.DMA((peers,)),
+        ],
+        compiler_params=pltpu.CompilerParams(collective_id=1, has_side_effects=True),
+    )(own)
+
+
 def per_device(g_less, g_ret, neighbors, ph_shift, q_table, coupling, occupation):
     edev = g_less.shape[1]
     width = g_less.shape[4]
@@ -120,11 +160,9 @@
     picked = jnp.einsum("enjrc,cp->enjpr", held, e4, preferred_element_type=jnp.float32)
     picked = picked.astype(jnp.bfloat16).reshape(edev, 2 * members * ORB, width)
 
-    window = padded(picked, "energy", 0, edev)
-    blocks = [window]
-    for d in range(1, xs):
-        blocks.append(lax.ppermute(window, "kz", [(i, (i + d * ZHI) % momenta) for i in range(momenta)]))
-    gathered = jnp.stack(blocks, 0)
+    rows = picked.shape[1]
+    gathered = gather(picked.reshape(edev * rows, width))
+    gathered = gathered.reshape(xs, 3 * edev, rows, width)
 
     me = lax.axis_index("kz")
     x = me // ZHI

time: 83.5 us -> 84.3 us (level)
  the two profiles are of different devices: /device:TPU:24 before, /device:TPU:1 now
where the time goes in v4:
time: 84.3 us; the launch traced here: 83.7 us
  Pallas kernels  62.3 us (74%)
  matrix products  6.79 us (8%)
  local copies, waits for them, and re-layouts  6.31 us (7%)
  between operations  6.28 us (7%)
  other arithmetic  2.1 us (2%)
    pallas_call x1, Pallas kernels, exchange(): pl.pallas_call(exchange_kernel, out_shape=jax.ShapeDtypeStruct((rows, lan...  39 us
    pallas_call x1, Pallas kernels, gather(): pl.pallas_call(gather_kernel, out_shape=jax.ShapeDtypeStruct((xs, 3) + ow...  23.2 us

profile of v4, /device:TPU:1, one launch (start us, length us, event | category | flops | bytes accessed | tf_op | source)
XLA Modules:
  0.0 83.7 jit_solution(10017643210972138488)
XLA Ops:
  0.0 0.0 copy-start
  0.0 0.9 %fusion.20 = f32[4,16]{1,0:T(4,128)S(1)} fusion(s32[16,16]{1,0:T(8,128)} %param.11, s32[4]{0:T(128)S(1)} %get-tuple-element.21), kind=kOutput, calls=%fused_computation.39 | convolution fusion | flops 12608 | bytes 1296 | tf_op jit(solution)/shard_map/dot_general | solution.py:31
  0.9 0.2 convolution_convert_fusion.1
  1.1 0.0 copy-done
  1.1 0.3 fusion.6
  1.4 1.3 %fusion.37 = (f32[1]{0:T(128)}, f32[1]{0:T(128)}) fusion(f32[2]{0:T(128)} %param.13), kind=kLoop, calls=%fused_computation.77 | loop fusion | bytes 16 | tf_op jit(solution)/shard_map/slice | solution.py:181
  3.9 1.2 %slice_multiply_fusion = (f32[1,4,4]{2,0,1:T(1,128)S(1)}, f32[1,4,4]{2,0,1:T(1,128)S(1)}, f32[1,4,4]{2,0,1:T(1,128)S(1)}, f32[1,4,4]{2,0,1:T(1,128)S(1)}) fusion(f32[2,4,4]{2,0,1:T(2,128)S(1)} %fusion.6, f32[]{:T(128)S(6)} %add.151, f32[]{:T(128)S(6)} %add.142, f32[]{:T(128)} %bitcast.21, f32[]{:T(128)} %bitcast.2), kind=kLoop, calls=%fused_computation.55 | loop fusion | flops 64 | bytes 400 | tf_op jit(solution)/shard_map/mul | solution.py:184
  5.2 1.3 %fusion.36 = (s32[1]{0:T(128)}, s32[1]{0:T(128)}) fusion(s32[2]{0:T(128)} %param.10), kind=kLoop, calls=%fused_computation.76 | loop fusion | bytes 16 | tf_op jit(solution)/shard_map/slice | solution.py:178
  7.0 0.0 copy-start.2
  11.4 0.7 pad_add_fusion
  12.1 0.1 broadcast_in_dim.2
  12.2 0.1 reshape.138
  12.3 0.2 fusion.19
  12.4 0.0 copy-done.2
  12.4 1.0 %convolution_convert_fusion = bf16[4,3,2,5,128]{4,0,3,2,1:T(4,128)(2,1)} fusion(bf16[5,128,128]{2,1,0:T(8,128)(2,1)S(1)} %get-tuple-element.10, bf16[3,2,128,128]{3,2,1,0:T(8,128)(2,1)S(1)} %bitcast.107, s32[128]{0:T(128)S(1)} %get-tuple-element.20), kind=kOutput, calls=%fused_computation.14 | convolution fusion | flops 5914112 | bytes 391680 | tf_op jit(solution)/shard_map/enjrc,cp->enjpr/dot_general | solution.py:160
  13.4 23.2 %shard_map.73 = bf16[4,3,120,128]{3,2,1,0:T(8,128)(2,1)} custom-call(bf16[120,128]{1,0:T(8,128)(2,1)} %bitcast.100), custom_call_target="tpu_custom_call" | custom-call | tf_op jit(solution)/shard_map/pallas_call | solution.py:135
  36.7 1.1 %constant_dynamic-slice_fusion = (bf16[4,3,40,128]{3,2,1,0:T(8,128)(2,1)S(1)}, bf16[4,3,40,128]{3,2,1,0:T(8,128)(2,1)S(1)}, bf16[4,3,40,128]{3,2,1,0:T(8,128)(2,1)S(1)}, bf16[4,3,40,128]{3,2,1,0:T(8,128)(2,1)S(1)}) fusion(bf16[4,9,40,128]{3,2,1,0:T(8,128)(2,1)} %bitcast.97, s32[]{:T(128)S(6)} %select_n.72, s32[]{:T(128)S(6)} %select_n.71, s32[]{:T(128)S(6)} %select_n.70, ...), kind=kLoop, calls=%fused_computation.63 | loop fusion | bytes 983056 | tf_op jit(solution)/shard_map/dynamic_slice | solution.py:179
  37.8 0.3 fusion.13
  38.2 0.4 convolution_add_fusion.2
  38.5 0.4 convolution_add_fusion.1
  38.9 0.4 convolution_add_fusion
  39.3 0.7 copy.34
  40.0 39.0 %shard_map.74 = bf16[120,128]{1,0:T(8,128)(2,1)} custom-call(f32[4,120,128]{2,1,0:T(8,128)} %bitcast.98), custom_call_target="tpu_custom_call" | custom-call | tf_op jit(solution)/shard_map/pallas_call | solution.py:83
  79.0 1.3 %multiply_reduce_fusion = bf16[3,2,128,128]{3,2,1,0:T(8,128)(2,1)S(1)} fusion(bf16[3,2,5,4,128]{4,3,2,1,0:T(4,128)(2,1)} %bitcast.99, f32[5,128,128]{2,1,0:T(8,128)S(1)} %get-tuple-element.9, s32[128]{0:T(128)S(1)} %get-tuple-element.20), kind=kOutput, calls=%fused_computation | convolution fusion | flops 4817408 | bytes 555520 | tf_op jit(solution)/shard_map/enjpr,cp->enjrc/dot_general | solution.py:190
  80.3 0.0 copy-start.1
  80.3 0.2 copy.35
  80.5 0.7 copy-done.1
  81.3 0.2 fusion.15
  81.5 0.2 fusion
  81.7 0.2 fusion.18
  81.9 0.2 fusion.16
  82.1 0.2 fusion.1
  82.3 0.2 fusion.5
  82.6 0.2 fusion.17
  82.8 0.2 fusion.4
  83.1 0.7 copy.41
  (5 shorter events, 0.1 us)
Async XLA Ops:
  0.0 1.1 %copy-start = (f32[2,16]{1,0:T(2,128)S(1)}, f32[2,16]{1,0:T(2,128)}, u32[]{:S(2)}) copy-start(f32[2,16]{1,0:T(2,128)} %param.12) | copy-start | bytes 388
  7.0 5.4 %copy-start.2 = (bf16[1,3,1,2,128,128]{5,4,3,2,1,0:T(8,128)(2,1)S(1)}, bf16[1,3,1,2,128,128]{5,4,3,2,1,0:T(8,128)(2,1)}, u32[]{:S(2)}) copy-start(bf16[1,3,1,2,128,128]{5,4,3,2,1,0:T(8,128)(2,1)} %param.7) | copy-start | bytes 589828
  80.3 0.9 %copy-start.1 = (bf16[1,3,1,1,2,128,128]{6,5,4,3,2,1,0:T(8,128)(2,1)S(1)}, bf16[1,3,1,1,2,128,128]{6,5,4,3,2,1,0:T(8,128)(2,1)}, u32[]{:S(2)}) copy-start(bf16[1,3,1,1,2,128,128]{6,5,4,3,2,1,0:T(8,128)(2,1)} %param.8) | copy-start | bytes 589828

commit v5 on v3

v5 whole, which is shorter than its diff:
```python
import jax
import jax.numpy as jnp
from jax import lax
from jax.experimental import pallas as pl
from jax.experimental.pallas import tpu as pltpu
from jax.sharding import PartitionSpec as P

ORB = 4
NMODE = 2
ZHI = 4


def masks(neighbors, width):
    atoms = width // ORB
    own = jnp.arange(atoms, dtype=jnp.int32)[:, None]
    pairs = jnp.concatenate([own, neighbors[0]], axis=1)
    row_pairs = jnp.repeat(pairs, ORB, axis=0)
    col_atom = jnp.arange(width, dtype=jnp.int32) // ORB
    return (row_pairs.T[:, :, None] == col_atom[None, None, :]).astype(jnp.bfloat16)


def spread(width):
    return (jnp.arange(width)[:, None] % ORB == jnp.arange(ORB)[None, :]).astype(jnp.bfloat16)


def born_kernel(own_ref, q_ref, c_ref, occ_ref, sh_ref, out_ref, land, part, relay_r, relay_l,
                near_r, near_l, far_r, far_l, sum_r, sum_l, gsend, grecv, send, recv):
    kz = lax.axis_index("kz")
    eb = lax.axis_index("energy")
    ne = lax.axis_size("energy")
    momenta = lax.axis_size("kz")
    xs = momenta // ZHI
    x = kz // ZHI
    h = kz % ZHI
    edev = own_ref.shape[0]
    rows = own_ref.shape[1]
    mesh = pl.DeviceIdType.MESH
    peers = [(d, t) for d in range(xs) for t in (-1, 0, 1) if (d, t) != (0, 0)]
    right = x * ZHI + (h + 1) % ZHI
    left = x * ZHI + (h + ZHI - 1) % ZHI

    def where(d, t):
        return {"kz": ((x + d) % xs) * ZHI + h, "energy": (eb + t + ne) % ne}

    barrier = pltpu.get_barrier_semaphore()
    for d, t in peers:
        pl.semaphore_signal(barrier, 1, device_id=where(d, t), device_id_type=mesh)
    for nb in (left, right):
        pl.semaphore_signal(barrier, 1, device_id={"kz": nb}, device_id_type=mesh)
    pl.semaphore_wait(barrier, len(peers) + 2)

    copies = []
    for i, (d, t) in enumerate(peers):
        c = pltpu.make_async_remote_copy(
            src_ref=own_ref, dst_ref=land.at[d, pl.ds((1 - t) * edev, edev)],
            send_sem=gsend.at[i], recv_sem=grecv.at[i], device_id=where(d, t), device_id_type=mesh,
        )
        c.start()
        copies.append(c)
    land[0, pl.ds(edev, edev)] = own_ref[...]
    for c in copies:
        c.wait()
    zero = jnp.zeros((xs, edev) + own_ref.shape[1:], own_ref.dtype)

    @pl.when(eb == 0)
    def _():
        land[:, pl.ds(0, edev)] = zero

    @pl.when(eb == ne - 1)
    def _():
        land[:, pl.ds(2 * edev, edev)] = zero

    shifts = [sh_ref[m] for m in range(NMODE)]
    for z in range(ZHI):
        k = x * ZHI + (h + z) % ZHI
        weights = []
        for d in range(xs):
            q = q_ref[k, ((x - d + xs) % xs) * ZHI + h]
            for m in range(NMODE):
                w = c_ref[m, q] / momenta
                weights.append((d, m, w * occ_ref[m], w * (occ_ref[m] + 1.0)))
        for e in range(edev):
            acc = jnp.zeros(own_ref.shape[1:], jnp.float32)
            for d, m, wl, wu in weights:
                acc = acc + wl * land[d, edev + e - shifts[m]].astype(jnp.float32)
                acc = acc + wu * land[d, edev + e + shifts[m]].astype(jnp.float32)
            part[z, pl.ds(e * rows, rows)] = acc

    half = part.shape[1] // 2
    lo = pl.ds(0, half)
    hi = pl.ds(half, half)

    def remote(src, dst, slot, to):
        return pltpu.make_async_remote_copy(
            src_ref=src, dst_ref=dst, send_sem=send.at[slot], recv_sem=recv.at[slot],
            device_id={"kz": to}, device_id_type=mesh,
        )

    far_right = remote(part.at[2, lo], relay_r, 0, right)
    far_left = remote(part.at[2, hi], relay_l, 1, left)
    plain_right = remote(part.at[1, hi], near_r, 2, right)
    plain_left = remote(part.at[ZHI - 1, lo], near_l, 3, left)
    for c in (far_right, far_left, plain_right, plain_left):
        c.start()
    far_right.wait_recv()
    sum_r[...] = relay_r[...] + part[1, lo]
    merged_right = remote(sum_r, far_r, 4, right)
    merged_right.start()
    far_left.wait_recv()
    sum_l[...] = relay_l[...] + part[ZHI - 1, hi]
    merged_left = remote(sum_l, far_l, 5, left)
    merged_left.start()
    plain_right.wait()
    plain_left.wait()
    far_right.wait_send()
    far_left.wait_send()
    merged_right.wait()
    merged_left.wait()
    out_ref[lo] = (part[0, lo] + near_l[...] + far_r[...]).astype(out_ref.dtype)
    out_ref[hi] = (part[0, hi] + near_r[...] + far_l[...]).astype(out_ref.dtype)


def born(own, q_table, coupling, occupation, ph_shift):
    edev, rows, lanes = own.shape
    xs = lax.axis_size("kz") // ZHI
    half = edev * rows // 2
    vmem = pltpu.VMEM
    smem = pl.BlockSpec(memory_space=pltpu.SMEM)
    return pl.pallas_call(
        born_kernel,
        out_shape=jax.ShapeDtypeStruct((edev * rows, lanes), jnp.bfloat16),
        in_specs=[pl.BlockSpec(memory_space=vmem), smem, smem, smem, smem],
        out_specs=pl.BlockSpec(memory_space=vmem),
        scratch_shapes=[
            vmem((xs, 3 * edev, rows, lanes), own.dtype),
            vmem((ZHI, edev * rows, lanes), jnp.float32),
        ]
        + [vmem((half, lanes), jnp.float32) for _ in range(8)]
        + [
            pltpu.SemaphoreType.DMA((3 * xs - 1,)),
            pltpu.SemaphoreType.DMA((3 * xs - 1,)),
            pltpu.SemaphoreType.DMA((6,)),
            pltpu.SemaphoreType.DMA((6,)),
        ],
        compiler_params=pltpu.CompilerParams(collective_id=0, has_side_effects=True),
    )(own, q_table, coupling, occupation, ph_shift)


def per_device(g_less, g_ret, neighbors, ph_shift, q_table, coupling, occupation):
    edev = g_less.shape[1]
    width = g_less.shape[4]
    members = neighbors.shape[2] + 1
    momenta = lax.axis_size("kz")
    xs = momenta // ZHI
    mask = masks(neighbors, width)
    e4 = spread(width)

    green = g_less[0, :, 0]
    held = green[:, :, None] * mask[None, None]
    picked = jnp.einsum("enjrc,cp->enjpr", held, e4, preferred_element_type=jnp.float32)
    picked = picked.astype(jnp.bfloat16).reshape(edev, 2 * members * ORB, width)
    sigma = born(picked, q_table, coupling, occupation, ph_shift)
    sigma = sigma.reshape(edev, 2, members, ORB, width)

    tiled = jnp.einsum("enjpr,cp->enjrc", sigma, e4, preferred_element_type=jnp.float32)
    dense = jnp.sum(tiled * mask[None, None].astype(jnp.float32), axis=2).astype(jnp.bfloat16)

    greenr = g_ret[0, :, 0, 0]
    green_re = greenr[:, 0]
    green_im = greenr[:, 1]
    sig_re = dense[:, 0]
    sig_im = dense[:, 1]
    prod_re = jnp.einsum("eij,ejk->eik", green_re, sig_re, preferred_element_type=jnp.float32)
    prod_re = prod_re - jnp.einsum("eij,ejk->eik", green_im, sig_im, preferred_element_type=jnp.float32)
    prod_im = jnp.einsum("eij,ejk->eik", green_re, sig_im, preferred_element_type=jnp.float32)
    prod_im = prod_im + jnp.einsum("eij,ejk->eik", green_im, sig_re, preferred_element_type=jnp.float32)
    prod_re = prod_re.astype(jnp.bfloat16)
    prod_im = prod_im.astype(jnp.bfloat16)
    real_part = jnp.einsum("eik,elk->eil", prod_re, green_re, preferred_element_type=jnp.float32)
    real_part = real_part + jnp.einsum("eik,elk->eil", prod_im, green_im, preferred_element_type=jnp.float32)
    imag_part = jnp.einsum("eik,elk->eil", prod_im, green_re, preferred_element_type=jnp.float32)
    imag_part = imag_part - jnp.einsum("eik,elk->eil", prod_re, green_im, preferred_element_type=jnp.float32)
    result = jnp.stack([real_part, imag_part], axis=1).astype(jnp.bfloat16)
    return result[None, :, None]


def solution(mesh):
    placed = (
        P("kz", "energy", None, None, None, None),
        P("kz", "energy", None, None, None, None, None),
        P(),
        P(),
        P(),
        P(),
        P(),
    )
    return jax.shard_map(
        per_device,
        mesh=mesh,
        in_specs=placed,
        out_specs=P("kz", "energy", None, None, None, None),
        check_vma=False,
    )
```

time: 83.5 us -> 63.9 us (0.77)
  starting transfers between devices: 26.2 us -> 0 us
  Pallas kernels: 37.7 us -> 55.8 us
  between operations: 7.02 us -> 0.09 us
  other arithmetic: 3.11 us -> 0.87 us
  matrix products: 5.46 us -> 3.99 us
    ppermute x5 -> x0, starting transfers between devices: 26.2 us -> none  [the longest x1 12.8 us: padded(): lax.ppermute(head, axis, [((i + 1) % count, i) for i in range(ends)])]
    pallas_call x1, Pallas kernels: 37.7 us -> 55.8 us  [born(): pl.pallas_call(born_kernel, out_shape=jax.ShapeDtypeStruct((edev * rows,...]
    dot_general x7 -> x0, matrix products: 2.09 us -> none  [the longest x2 0.71 us: per_device(): jnp.einsum('zd,derb->zerb', weights[mode] * (occupation[mode] + 1.0), upp...]
    unnamed x13 -> x3, local copies, waits for them, and re-layouts: 0.04 us -> 1.71 us
    mul x1 -> x0, other arithmetic: 1.29 us -> none  [per_device(): weights[mode] * (occupation[mode] + 1.0)]
    slice x2 -> x0, local copies, waits for them, and re-layouts: 1.18 us -> none  [the longest x1 0.59 us: per_device(): ph_shift[mode]]
    another operation x2 -> x0, other arithmetic: 0.89 us -> none  [per_device(): gathered = jnp.stack(blocks, 0)]
  transfers between devices with their start and end apart: 5 -> 0, of which waited for: 0 -> 0; matrix products, arithmetic and copies ran while one was open for 4% -> 0% of each run, Pallas kernels for 0% -> 0%
where the time goes in v5:
time: 63.9 us; the launch traced here: 63.5 us
  Pallas kernels  55.8 us (87%)
  matrix products  3.99 us (6%)
  local copies, waits for them, and re-layouts  2.76 us (4%)
  other arithmetic  0.87 us (1%)
    pallas_call x1, Pallas kernels, born(): pl.pallas_call(born_kernel, out_shape=jax.ShapeDtypeStruct((edev * rows,...  55.8 us
    unnamed x3, local copies, waits for them, and re-layouts  1.71 us

profile of v5, /device:TPU:24, one launch (start us, length us, event | category | flops | bytes accessed | tf_op | source)
XLA Modules:
  0.0 63.5 jit_solution(9224478672156182049)
XLA Ops:
  0.0 0.7 %pad_add_fusion = s32[32,5]{0,1:T(8,128)S(1)} fusion(s32[32,4]{0,1:T(4,128)} %bitcast.58, s32[32,1]{0,1:T(1,128)S(1)} %iota.23), kind=kLoop, calls=%fused_computation.27 | loop fusion | flops 160 | bytes 1280 | tf_op jit(solution)/shard_map/concatenate | solution.py:16
  0.7 0.1 broadcast_in_dim.2
  0.8 0.1 reshape.77
  0.9 0.9 %copy.33 = bf16[1,3,1,1,2,128,128]{6,5,1,4,3,2,0:T(8,128)(2,1)S(1)} copy(bf16[1,3,1,1,2,128,128]{6,5,4,3,2,1,0:T(8,128)(2,1)} %param.8) | data formatting | bytes 393216 | tf_op args[1]
  1.8 0.0 copy-start
  1.9 0.2 fusion.13
  2.0 0.8 %copy-done = bf16[1,3,1,2,128,128]{5,4,3,2,1,0:T(8,128)(2,1)S(1)} copy-done((bf16[1,3,1,2,128,128]{5,4,3,2,1,0:T(8,128)(2,1)S(1)}, bf16[1,3,1,2,128,128]{5,4,3,2,1,0:T(8,128)(2,1)}, u32[]{:S(2)}) %copy-start) | copy-done | bytes 196632
  2.8 1.0 %convolution_convert_fusion = bf16[4,3,2,5,128]{4,0,3,2,1:T(4,128)(2,1)} fusion(bf16[5,128,128]{2,1,0:T(8,128)(2,1)S(1)} %get-tuple-element.6, bf16[3,2,128,128]{3,2,1,0:T(8,128)(2,1)S(1)} %bitcast.59, s32[128]{0:T(128)S(1)} %and_select_fusion.1), kind=kOutput, calls=%fused_computation.11 | convolution fusion | flops 5914112 | bytes 391680 | tf_op jit(solution)/shard_map/enjrc,cp->enjpr/dot_general | solution.py:160
  3.8 55.8 %shard_map.73 = bf16[120,128]{1,0:T(8,128)(2,1)} custom-call(bf16[3,40,128]{2,1,0:T(8,128)(2,1)} %bitcast.56, s32[16,16]{1,0:T(8,128)} %q_ref.1, f32[2,16]{1,0:T(2,128)} %c_ref.1, f32[2]{0:T(128)} %occ_ref.1, s32[2]{0:T(128)} %sh_ref.1), custom_call_target="tpu_custom_call" | custom-call | tf_op jit(solution)/shard_map/pallas_call | solution.py:129
  59.5 1.3 %multiply_reduce_fusion = bf16[3,2,128,128]{3,2,1,0:T(8,128)(2,1)S(1)} fusion(bf16[3,2,5,4,128]{4,3,2,1,0:T(4,128)(2,1)} %bitcast.55, f32[5,128,128]{2,1,0:T(8,128)S(1)} %get-tuple-element.5, s32[128]{0:T(128)S(1)} %and_select_fusion.1), kind=kOutput, calls=%fused_computation | convolution fusion | flops 4817408 | bytes 555520 | tf_op jit(solution)/shard_map/enjpr,cp->enjrc/dot_general | solution.py:165
  60.8 0.2 copy.20
  61.0 0.2 fusion.9
  61.2 0.2 fusion
  61.4 0.2 fusion.12
  61.6 0.2 fusion.10
  61.8 0.2 fusion.1
  62.0 0.2 fusion.5
  62.3 0.2 fusion.11
  62.5 0.2 fusion.4
  62.8 0.7 %copy.26 = bf16[1,3,1,2,128,128]{5,4,3,2,1,0:T(8,128)(2,1)} copy(bf16[1,3,1,2,128,128]{5,4,1,3,2,0:T(8,128)(2,1)S(1)} %pad_maximum_fusion) | data formatting | bytes 393216 | tf_op jit(solution)/shard_map/stack | solution.py:183
  (4 shorter events, 0.0 us)
Async XLA Ops:
  1.8 0.9 %copy-start = (bf16[1,3,1,2,128,128]{5,4,3,2,1,0:T(8,128)(2,1)S(1)}, bf16[1,3,1,2,128,128]{5,4,3,2,1,0:T(8,128)(2,1)}, u32[]{:S(2)}) copy-start(bf16[1,3,1,2,128,128]{5,4,3,2,1,0:T(8,128)(2,1)} %param.7) | copy-start | bytes 589828

commit v6 on v5

--- a/solution.py
+++ b/solution.py
@@ -23,7 +23,7 @@
     return (jnp.arange(width)[:, None] % ORB == jnp.arange(ORB)[None, :]).astype(jnp.bfloat16)
 
 
-def born_kernel(own_ref, q_ref, c_ref, occ_ref, sh_ref, out_ref, land, part, relay_r, relay_l,
+def born_kernel(own_ref, q_ref, c_ref, occ_ref, sh_ref, out_ref, land, landf, part, relay_r, relay_l,
                 near_r, near_l, far_r, far_l, sum_r, sum_l, gsend, grecv, send, recv):
     kz = lax.axis_index("kz")
     eb = lax.axis_index("energy")
@@ -57,21 +57,21 @@
         )
         c.start()
         copies.append(c)
-    land[0, pl.ds(edev, edev)] = own_ref[...]
+    for e in range(edev):
+        landf[0, edev + e] = own_ref[e].astype(jnp.float32)
     for c in copies:
         c.wait()
-    zero = jnp.zeros((xs, edev) + own_ref.shape[1:], own_ref.dtype)
-
-    @pl.when(eb == 0)
-    def _():
-        land[:, pl.ds(0, edev)] = zero
-
-    @pl.when(eb == ne - 1)
-    def _():
-        land[:, pl.ds(2 * edev, edev)] = zero
+    keep = (jnp.where(eb > 0, 1.0, 0.0), 1.0, jnp.where(eb < ne - 1, 1.0, 0.0))
+    for d in range(xs):
+        for side in range(3):
+            if (d, side) == (0, 1):
+                continue
+            for e in range(edev):
+                landf[d, side * edev + e] = land[d, side * edev + e].astype(jnp.float32) * keep[side]
 
     shifts = [sh_ref[m] for m in range(NMODE)]
-    for z in range(ZHI):
+
+    def partial(z):
         k = x * ZHI + (h + z) % ZHI
         weights = []
         for d in range(xs):
@@ -82,13 +82,9 @@
         for e in range(edev):
             acc = jnp.zeros(own_ref.shape[1:], jnp.float32)
             for d, m, wl, wu in weights:
-                acc = acc + wl * land[d, edev + e - shifts[m]].astype(jnp.float32)
-                acc = acc + wu * land[d, edev + e + shifts[m]].astype(jnp.float32)
+                acc = acc + wl * landf[d, edev + e - shifts[m]]
+                acc = acc + wu * landf[d, edev + e + shifts[m]]
             part[z, pl.ds(e * rows, rows)] = acc
-
-    half = part.shape[1] // 2
-    lo = pl.ds(0, half)
-    hi = pl.ds(half, half)
 
     def remote(src, dst, slot, to):
         return pltpu.make_async_remote_copy(
@@ -96,26 +92,47 @@
             device_id={"kz": to}, device_id_type=mesh,
         )
 
-    far_right = remote(part.at[2, lo], relay_r, 0, right)
-    far_left = remote(part.at[2, hi], relay_l, 1, left)
-    plain_right = remote(part.at[1, hi], near_r, 2, right)
-    plain_left = remote(part.at[ZHI - 1, lo], near_l, 3, left)
-    for c in (far_right, far_left, plain_right, plain_left):
-        c.start()
-    far_right.wait_recv()
-    sum_r[...] = relay_r[...] + part[1, lo]
-    merged_right = remote(sum_r, far_r, 4, right)
-    merged_right.start()
-    far_left.wait_recv()
-    sum_l[...] = relay_l[...] + part[ZHI - 1, hi]
-    merged_left = remote(sum_l, far_l, 5, left)
-    merged_left.start()
+    total = part.shape[1]
+    split = relay_r.shape[0]
+    step = split // 2
+    chunks_r = [(0, step), (step, split - step)]
+    chunks_l = [(0, step), (step, total - split - step)]
+    partial(2)
+    far_right = [remote(part.at[2, pl.ds(o, n)], relay_r.at[pl.ds(o, n)], i, right)
+                 for i, (o, n) in enumerate(chunks_r)]
+    far_left = [remote(part.at[2, pl.ds(split + o, n)], relay_l.at[pl.ds(o, n)], 2 + i, left)
+                for i, (o, n) in enumerate(chunks_l)]
+    for c in far_right + far_left:
+        c.start()
+    partial(1)
+    plain_right = remote(part.at[1, pl.ds(split, total - split)], near_r, 4, right)
+    plain_right.start()
+    partial(ZHI - 1)
+    plain_left = remote(part.at[ZHI - 1, pl.ds(0, split)], near_l, 5, left)
+    plain_left.start()
+    partial(0)
+    merged = []
+    for i in range(2):
+        o, n = chunks_r[i]
+        far_right[i].wait_recv()
+        sum_r[pl.ds(o, n)] = relay_r[pl.ds(o, n)] + part[1, pl.ds(o, n)]
+        c = remote(sum_r.at[pl.ds(o, n)], far_r.at[pl.ds(o, n)], 6 + i, right)
+        c.start()
+        merged.append(c)
+        o, n = chunks_l[i]
+        far_left[i].wait_recv()
+        sum_l[pl.ds(o, n)] = relay_l[pl.ds(o, n)] + part[ZHI - 1, pl.ds(split + o, n)]
+        c = remote(sum_l.at[pl.ds(o, n)], far_l.at[pl.ds(o, n)], 8 + i, left)
+        c.start()
+        merged.append(c)
     plain_right.wait()
     plain_left.wait()
-    far_right.wait_send()
-    far_left.wait_send()
-    merged_right.wait()
-    merged_left.wait()
+    for c in far_right + far_left:
+        c.wait_send()
+    for c in merged:
+        c.wait()
+    lo = pl.ds(0, split)
+    hi = pl.ds(split, total - split)
     out_ref[lo] = (part[0, lo] + near_l[...] + far_r[...]).astype(out_ref.dtype)
     out_ref[hi] = (part[0, hi] + near_r[...] + far_l[...]).astype(out_ref.dtype)
 
@@ -123,24 +140,32 @@
 def born(own, q_table, coupling, occupation, ph_shift):
     edev, rows, lanes = own.shape
     xs = lax.axis_size("kz") // ZHI
-    half = edev * rows // 2
+    total = edev * rows
+    split = (total // 2 + 15) // 16 * 16
     vmem = pltpu.VMEM
     smem = pl.BlockSpec(memory_space=pltpu.SMEM)
+    f32 = jnp.float32
     return pl.pallas_call(
         born_kernel,
-        out_shape=jax.ShapeDtypeStruct((edev * rows, lanes), jnp.bfloat16),
+        out_shape=jax.ShapeDtypeStruct((total, lanes), jnp.bfloat16),
         in_specs=[pl.BlockSpec(memory_space=vmem), smem, smem, smem, smem],
         out_specs=pl.BlockSpec(memory_space=vmem),
         scratch_shapes=[
             vmem((xs, 3 * edev, rows, lanes), own.dtype),
-            vmem((ZHI, edev * rows, lanes), jnp.float32),
-        ]
-        + [vmem((half, lanes), jnp.float32) for _ in range(8)]
-        + [
+            vmem((xs, 3 * edev, rows, lanes), f32),
+            vmem((ZHI, total, lanes), f32),
+            vmem((split, lanes), f32),
+            vmem((total - split, lanes), f32),
+            vmem((total - split, lanes), f32),
+            vmem((split, lanes), f32),
+            vmem((split, lanes), f32),
+            vmem((total - split, lanes), f32),
+            vmem((split, lanes), f32),
+            vmem((total - split, lanes), f32),
             pltpu.SemaphoreType.DMA((3 * xs - 1,)),
             pltpu.SemaphoreType.DMA((3 * xs - 1,)),
-            pltpu.SemaphoreType.DMA((6,)),
-            pltpu.SemaphoreType.DMA((6,)),
+            pltpu.SemaphoreType.DMA((10,)),
+            pltpu.SemaphoreType.DMA((10,)),
         ],
         compiler_params=pltpu.CompilerParams(collective_id=0, has_side_effects=True),
     )(own, q_table, coupling, occupation, ph_shift)

time: 63.9 us -> 63.6 us (level)
  Pallas kernels: 55.8 us -> 55.1 us
where the time goes in v6:
time: 63.6 us; the launch traced here: 62.8 us
  Pallas kernels  55.1 us (87%)
  matrix products  4 us (6%)
  local copies, waits for them, and re-layouts  2.76 us (4%)
  other arithmetic  0.87 us (1%)
    pallas_call x1, Pallas kernels, born(): pl.pallas_call(born_kernel, out_shape=jax.ShapeDtypeStruct((total, lanes)...  55.1 us
    unnamed x3, local copies, waits for them, and re-layouts  1.71 us

profile of v6, /device:TPU:24, one launch (start us, length us, event | category | flops | bytes accessed | tf_op | source)
XLA Modules:
  0.0 62.8 jit_solution(12305595623986056503)
XLA Ops:
  0.0 0.7 %pad_add_fusion = s32[32,5]{0,1:T(8,128)S(1)} fusion(s32[32,4]{0,1:T(4,128)} %bitcast.58, s32[32,1]{0,1:T(1,128)S(1)} %iota.23), kind=kLoop, calls=%fused_computation.27 | loop fusion | flops 160 | bytes 1280 | tf_op jit(solution)/shard_map/concatenate | solution.py:16
  0.7 0.1 broadcast_in_dim.2
  0.8 0.1 reshape.77
  0.9 0.9 %copy.33 = bf16[1,3,1,1,2,128,128]{6,5,1,4,3,2,0:T(8,128)(2,1)S(1)} copy(bf16[1,3,1,1,2,128,128]{6,5,4,3,2,1,0:T(8,128)(2,1)} %param.8) | data formatting | bytes 393216 | tf_op args[1]
  1.8 0.0 copy-start
  1.9 0.2 fusion.13
  2.0 0.8 %copy-done = bf16[1,3,1,2,128,128]{5,4,3,2,1,0:T(8,128)(2,1)S(1)} copy-done((bf16[1,3,1,2,128,128]{5,4,3,2,1,0:T(8,128)(2,1)S(1)}, bf16[1,3,1,2,128,128]{5,4,3,2,1,0:T(8,128)(2,1)}, u32[]{:S(2)}) %copy-start) | copy-done | bytes 196632
  2.8 1.0 %convolution_convert_fusion = bf16[4,3,2,5,128]{4,0,3,2,1:T(4,128)(2,1)} fusion(bf16[5,128,128]{2,1,0:T(8,128)(2,1)S(1)} %get-tuple-element.6, bf16[3,2,128,128]{3,2,1,0:T(8,128)(2,1)S(1)} %bitcast.59, s32[128]{0:T(128)S(1)} %and_select_fusion.1), kind=kOutput, calls=%fused_computation.11 | convolution fusion | flops 5914112 | bytes 391680 | tf_op jit(solution)/shard_map/enjrc,cp->enjpr/dot_general | solution.py:185
  3.8 55.1 %shard_map.73 = bf16[120,128]{1,0:T(8,128)(2,1)} custom-call(bf16[3,40,128]{2,1,0:T(8,128)(2,1)} %bitcast.56, s32[16,16]{1,0:T(8,128)} %q_ref.1, f32[2,16]{1,0:T(2,128)} %c_ref.1, f32[2]{0:T(128)} %occ_ref.1, s32[2]{0:T(128)} %sh_ref.1), custom_call_target="tpu_custom_call" | custom-call | tf_op jit(solution)/shard_map/pallas_call | solution.py:148
  58.9 1.3 %multiply_reduce_fusion = bf16[3,2,128,128]{3,2,1,0:T(8,128)(2,1)S(1)} fusion(bf16[3,2,5,4,128]{4,3,2,1,0:T(4,128)(2,1)} %bitcast.55, f32[5,128,128]{2,1,0:T(8,128)S(1)} %get-tuple-element.5, s32[128]{0:T(128)S(1)} %and_select_fusion.1), kind=kOutput, calls=%fused_computation | convolution fusion | flops 4817408 | bytes 555520 | tf_op jit(solution)/shard_map/enjpr,cp->enjrc/dot_general | solution.py:190
  60.2 0.2 copy.20
  60.4 0.2 fusion.9
  60.6 0.2 fusion
  60.8 0.2 fusion.12
  61.0 0.2 fusion.10
  61.2 0.2 fusion.1
  61.4 0.2 fusion.5
  61.7 0.2 fusion.11
  61.9 0.2 fusion.4
  62.2 0.7 %copy.26 = bf16[1,3,1,2,128,128]{5,4,3,2,1,0:T(8,128)(2,1)} copy(bf16[1,3,1,2,128,128]{5,4,1,3,2,0:T(8,128)(2,1)S(1)} %pad_maximum_fusion) | data formatting | bytes 393216 | tf_op jit(solution)/shard_map/stack | solution.py:208
  (4 shorter events, 0.0 us)
Async XLA Ops:
  1.8 0.9 %copy-start = (bf16[1,3,1,2,128,128]{5,4,3,2,1,0:T(8,128)(2,1)S(1)}, bf16[1,3,1,2,128,128]{5,4,3,2,1,0:T(8,128)(2,1)}, u32[]{:S(2)}) copy-start(bf16[1,3,1,2,128,128]{5,4,3,2,1,0:T(8,128)(2,1)} %param.7) | copy-start | bytes 589828

commit v7 on v6

--- a/solution.py
+++ b/solution.py
@@ -171,6 +171,42 @@
     )(own, q_table, coupling, occupation, ph_shift)
 
 
+def keldysh_kernel(sig_ref, green_ref, sel_ref, maskt_ref, out_ref):
+    f32 = jnp.float32
+    edev = green_ref.shape[0]
+    rows = sig_ref.shape[0] // edev
+    members = maskt_ref.shape[0]
+
+    def nt(a, b):
+        return lax.dot_general(a, b, (((1,), (1,)), ((), ())), preferred_element_type=f32)
+
+    for e in range(edev):
+        sig = sig_ref[pl.ds(e * rows, rows), :]
+        dense_t = []
+        for n in range(2):
+            acc = jnp.zeros(green_ref.shape[2:], f32)
+            for j in range(members):
+                tiled = jnp.dot(sel_ref[n * members + j], sig, preferred_element_type=f32)
+                acc = acc + tiled * maskt_ref[j].astype(f32)
+            dense_t.append(acc.astype(sig.dtype))
+        gr = green_ref[e, 0]
+        gi = green_ref[e, 1]
+        pr = (nt(gr, dense_t[0]) - nt(gi, dense_t[1])).astype(gr.dtype)
+        pi = (nt(gr, dense_t[1]) + nt(gi, dense_t[0])).astype(gr.dtype)
+        out_ref[e, 0] = (nt(pr, gr) + nt(pi, gi)).astype(out_ref.dtype)
+        out_ref[e, 1] = (nt(pi, gr) - nt(pr, gi)).astype(out_ref.dtype)
+
+
+def keldysh(sigma, green, sel, maskt):
+    vmem = pl.BlockSpec(memory_space=pltpu.VMEM)
+    return pl.pallas_call(
+        keldysh_kernel,
+        out_shape=jax.ShapeDtypeStruct(green.shape, jnp.bfloat16),
+        in_specs=[vmem, vmem, vmem, vmem],
+        out_specs=vmem,
+    )(sigma, green, sel, maskt)
+
+
 def per_device(g_less, g_ret, neighbors, ph_shift, q_table, coupling, occupation):
     edev = g_less.shape[1]
     width = g_less.shape[4]
@@ -185,27 +221,15 @@
     picked = jnp.einsum("enjrc,cp->enjpr", held, e4, preferred_element_type=jnp.float32)
     picked = picked.astype(jnp.bfloat16).reshape(edev, 2 * members * ORB, width)
     sigma = born(picked, q_table, coupling, occupation, ph_shift)
-    sigma = sigma.reshape(edev, 2, members, ORB, width)
-
-    tiled = jnp.einsum("enjpr,cp->enjrc", sigma, e4, preferred_element_type=jnp.float32)
-    dense = jnp.sum(tiled * mask[None, None].astype(jnp.float32), axis=2).astype(jnp.bfloat16)
-
-    greenr = g_ret[0, :, 0, 0]
-    green_re = greenr[:, 0]
-    green_im = greenr[:, 1]
-    sig_re = dense[:, 0]
-    sig_im = dense[:, 1]
-    prod_re = jnp.einsum("eij,ejk->eik", green_re, sig_re, preferred_element_type=jnp.float32)
-    prod_re = prod_re - jnp.einsum("eij,ejk->eik", green_im, sig_im, preferred_element_type=jnp.float32)
-    prod_im = jnp.einsum("eij,ejk->eik", green_re, sig_im, preferred_element_type=jnp.float32)
-    prod_im = prod_im + jnp.einsum("eij,ejk->eik", green_im, sig_re, preferred_element_type=jnp.float32)
-    prod_re = prod_re.astype(jnp.bfloat16)
-    prod_im = prod_im.astype(jnp.bfloat16)
-    real_part = jnp.einsum("eik,elk->eil", prod_re, green_re, preferred_element_type=jnp.float32)
-    real_part = real_part + jnp.einsum("eik,elk->eil", prod_im, green_im, preferred_element_type=jnp.float32)
-    imag_part = jnp.einsum("eik,elk->eil", prod_im, green_re, preferred_element_type=jnp.float32)
-    imag_part = imag_part - jnp.einsum("eik,elk->eil", prod_re, green_im, preferred_element_type=jnp.float32)
-    result = jnp.stack([real_part, imag_part], axis=1).astype(jnp.bfloat16)
+
+    row = jnp.arange(2 * members * ORB)[None, :]
+    col = jnp.arange(width)[:, None]
+    sel = jnp.stack([
+        (row // (members * ORB) == n) & ((row // ORB) % members == j) & (row % ORB == col % ORB)
+        for n in range(2) for j in range(members)
+    ]).astype(jnp.bfloat16)
+    maskt = jnp.swapaxes(mask, 1, 2)
+    result = keldysh(sigma, g_ret[0, :, 0, 0], sel, maskt)
     return result[None, :, None]
 
 

time: 63.6 us -> 63.9 us (level)
  Pallas kernels: 55.1 us -> 58.5 us
  matrix products: 4 us -> 1 us
  local copies, waits for them, and re-layouts: 2.76 us -> 1.1 us
  other arithmetic: 0.87 us -> 2.51 us
    pallas_call x0 -> x1, Pallas kernels: none -> 3.37 us  [keldysh(): pl.pallas_call(keldysh_kernel, out_shape=jax.ShapeDtypeStruct(green.shape...]
    dot_general x9 -> x0, matrix products: 3 us -> none  [the longest x1 1.27 us: per_device(): jnp.einsum('enjpr,cp->enjrc', sigma, e4, preferred_element_type=jnp.float32)]
    unnamed x3 -> x2, local copies, waits for them, and re-layouts: 1.71 us -> 0.01 us
    convert_element_type x0 -> x1, local copies, waits for them, and re-layouts: none -> 0.9 us  [per_device(): sel = jnp.stack([(row // (members * ORB) == n) & (row // ORB % members ==...]
    unnamed x0 -> x9, other arithmetic: none -> 0.75 us
    another operation x1 -> x0, local copies, waits for them, and re-layouts: 0.69 us -> none  [per_device(): result = jnp.stack([real_part, imag_part], axis=1).astype(jnp.bfloat16)]
    convert_element_type x1 -> x2, other arithmetic: 0.15 us -> 0.83 us  [the longest x1 0.81 us: masks(): (row_pairs.T[:, :, None] == col_atom[None, None, :]).astype(jnp.bfloat16)]
where the time goes in v7:
time: 63.9 us; the launch traced here: 63.2 us
  Pallas kernels  58.5 us (92%)
  other arithmetic  2.51 us (4%)
  local copies, waits for them, and re-layouts  1.1 us (2%)
  matrix products  1 us (2%)
    pallas_call x1, Pallas kernels, born(): pl.pallas_call(born_kernel, out_shape=jax.ShapeDtypeStruct((total, lanes)...  55.1 us
    pallas_call x1, Pallas kernels, keldysh(): pl.pallas_call(keldysh_kernel, out_shape=jax.ShapeDtypeStruct(green.shape...  3.37 us

profile of v7, /device:TPU:24, one launch (start us, length us, event | category | flops | bytes accessed | tf_op | source)
XLA Modules:
  0.0 63.2 jit_solution(9504885112484783091)
XLA Ops:
  0.2 0.7 %pad_add_fusion = s32[32,5]{0,1:T(8,128)S(1)} fusion(s32[32,4]{0,1:T(4,128)} %bitcast.20, s32[32,1]{0,1:T(1,128)S(1)} %iota.79), kind=kLoop, calls=%fused_computation.26 | loop fusion | flops 160 | bytes 1280 | tf_op jit(solution)/shard_map/concatenate | solution.py:16
  0.9 0.1 constant_dynamic-update-slice_fusion.9
  1.0 0.1 constant_dynamic-update-slice_fusion.8
  1.1 0.1 constant_dynamic-update-slice_fusion.7
  1.2 0.1 constant_dynamic-update-slice_fusion.6
  1.2 0.1 constant_dynamic-update-slice_fusion.5
  1.3 0.1 constant_dynamic-update-slice_fusion.4
  1.4 0.1 constant_dynamic-update-slice_fusion.3
  1.5 0.1 constant_dynamic-update-slice_fusion.2
  1.6 0.1 constant_dynamic-update-slice_fusion.1
  1.7 0.1 constant_dynamic-update-slice_fusion
  1.8 0.1 broadcast_in_dim.4
  1.9 0.1 reshape.806
  2.0 0.0 copy-start
  2.0 0.9 %copy.12.sel_ref = bf16[10,128,40]{2,1,0:T(8,128)(2,1)} copy(bf16[10,128,40]{1,2,0:T(8,128)(2,1)S(1)} %convert_element_type.23) | data formatting | bytes 204800 | tf_op jit(solution)/shard_map/convert_element_type | solution.py:230
  2.9 0.8 %compare_convert_fusion = (bf16[5,128,128]{2,1,0:T(8,128)(2,1)}, bf16[5,128,128]{2,1,0:T(8,128)(2,1)S(1)}) fusion(s32[5,128]{1,0:T(8,128)S(1)} %bitcast.18, s32[128]{0:T(128)S(1)} %and_select_fusion.4), kind=kLoop, calls=%fused_computation.4 | loop fusion | flops 327680 | bytes 330752 | tf_op jit(solution)/shard_map/convert_element_type | solution.py:19
  3.7 0.0 copy-done
  3.7 1.0 %convolution_convert_fusion = bf16[4,3,2,5,128]{4,0,3,2,1:T(4,128)(2,1)} fusion(bf16[5,128,128]{2,1,0:T(8,128)(2,1)S(1)} %get-tuple-element.6, bf16[3,2,128,128]{3,2,1,0:T(8,128)(2,1)S(1)} %bitcast.21, s32[128]{0:T(128)S(1)} %and_select_fusion.5), kind=kOutput, calls=%fused_computation | convolution fusion | flops 5914112 | bytes 391680 | tf_op jit(solution)/shard_map/enjrc,cp->enjpr/dot_general | solution.py:221
  4.7 55.1 %shard_map.73.sig_ref = bf16[120,128]{1,0:T(8,128)(2,1)} custom-call(bf16[3,40,128]{2,1,0:T(8,128)(2,1)} %bitcast.19, s32[16,16]{1,0:T(8,128)} %q_ref.1, f32[2,16]{1,0:T(2,128)} %c_ref.1, f32[2]{0:T(128)} %occ_ref.1, s32[2]{0:T(128)} %sh_ref.1), custom_call_target="tpu_custom_call" | custom-call | tf_op jit(solution)/shard_map/pallas_call | solution.py:148
  59.9 3.4 %shard_map.74 = bf16[3,2,128,128]{3,2,1,0:T(8,128)(2,1)} custom-call(bf16[120,128]{1,0:T(8,128)(2,1)} %shard_map.73.sig_ref, bf16[3,2,128,128]{3,2,1,0:T(8,128)(2,1)} %bitcast.17, bf16[10,128,40]{2,1,0:T(8,128)(2,1)} %copy.12.sel_ref, bf16[5,128,128]{2,1,0:T(8,128)(2,1)} %get-tuple-element.5.maskt_ref), custom_call_target="tpu_custom_call" | custom-call | tf_op jit(solution)/shard_map/pallas_call | solution.py:202
  (15 shorter events, 0.2 us)
Async XLA Ops:
  2.0 1.7 %copy-start = (bf16[1,3,1,2,128,128]{5,4,3,2,1,0:T(8,128)(2,1)S(1)}, bf16[1,3,1,2,128,128]{5,4,3,2,1,0:T(8,128)(2,1)}, u32[]{:S(2)}) copy-start(bf16[1,3,1,2,128,128]{5,4,3,2,1,0:T(8,128)(2,1)} %param.7) | copy-start | bytes 589828

commit v8 on v7

--- a/solution.py
+++ b/solution.py
@@ -171,11 +171,17 @@
     )(own, q_table, coupling, occupation, ph_shift)
 
 
-def keldysh_kernel(sig_ref, green_ref, sel_ref, maskt_ref, out_ref):
+def keldysh_kernel(sig_ref, green_ref, maskt_ref, out_ref):
     f32 = jnp.float32
     edev = green_ref.shape[0]
     rows = sig_ref.shape[0] // edev
     members = maskt_ref.shape[0]
+    width = green_ref.shape[2]
+    lane = lax.broadcasted_iota(jnp.int32, (width, rows), 1)
+    spread = lax.broadcasted_iota(jnp.int32, (width, rows), 0) & (ORB - 1)
+
+    def sel(base):
+        return jnp.where(lane - base == spread, 1.0, 0.0).astype(sig_ref.dtype)
 
     def nt(a, b):
         return lax.dot_general(a, b, (((1,), (1,)), ((), ())), preferred_element_type=f32)
@@ -186,7 +192,7 @@
         for n in range(2):
             acc = jnp.zeros(green_ref.shape[2:], f32)
             for j in range(members):
-                tiled = jnp.dot(sel_ref[n * members + j], sig, preferred_element_type=f32)
+                tiled = jnp.dot(sel((n * members + j) * ORB), sig, preferred_element_type=f32)
                 acc = acc + tiled * maskt_ref[j].astype(f32)
             dense_t.append(acc.astype(sig.dtype))
         gr = green_ref[e, 0]
@@ -197,14 +203,14 @@
         out_ref[e, 1] = (nt(pi, gr) - nt(pr, gi)).astype(out_ref.dtype)
 
 
-def keldysh(sigma, green, sel, maskt):
+def keldysh(sigma, green, maskt):
     vmem = pl.BlockSpec(memory_space=pltpu.VMEM)
     return pl.pallas_call(
         keldysh_kernel,
         out_shape=jax.ShapeDtypeStruct(green.shape, jnp.bfloat16),
-        in_specs=[vmem, vmem, vmem, vmem],
+        in_specs=[vmem, vmem, vmem],
         out_specs=vmem,
-    )(sigma, green, sel, maskt)
+    )(sigma, green, maskt)
 
 
 def per_device(g_less, g_ret, neighbors, ph_shift, q_table, coupling, occupation):
@@ -222,14 +228,9 @@
     picked = picked.astype(jnp.bfloat16).reshape(edev, 2 * members * ORB, width)
     sigma = born(picked, q_table, coupling, occupation, ph_shift)
 
-    row = jnp.arange(2 * members * ORB)[None, :]
-    col = jnp.arange(width)[:, None]
-    sel = jnp.stack([
-        (row // (members * ORB) == n) & ((row // ORB) % members == j) & (row % ORB == col % ORB)
-        for n in range(2) for j in range(members)
-    ]).astype(jnp.bfloat16)
-    maskt = jnp.swapaxes(mask, 1, 2)
-    result = keldysh(sigma, g_ret[0, :, 0, 0], sel, maskt)
+    sigma, later = lax.optimization_barrier((sigma, neighbors))
+    maskt = jnp.swapaxes(masks(later, width), 1, 2)
+    result = keldysh(sigma, g_ret[0, :, 0, 0], maskt)
     return result[None, :, None]
 
 

time: 63.9 us -> 62.2 us (0.973)
  other arithmetic: 2.51 us -> 1.65 us
  local copies, waits for them, and re-layouts: 1.1 us -> 0.38 us
    convert_element_type x1 -> x0, local copies, waits for them, and re-layouts: 0.9 us -> none  [per_device(): sel = jnp.stack([(row // (members * ORB) == n) & (row // ORB % members ==...]
    unnamed x9 -> x0, other arithmetic: 0.75 us -> none
where the time goes in v8:
time: 62.2 us; the launch traced here: 61.5 us
  Pallas kernels  58.4 us (94%)
  other arithmetic  1.65 us (3%)
  matrix products  1 us (2%)
    pallas_call x1, Pallas kernels, born(): pl.pallas_call(born_kernel, out_shape=jax.ShapeDtypeStruct((total, lanes)...  55.1 us
    pallas_call x1, Pallas kernels, keldysh(): pl.pallas_call(keldysh_kernel, out_shape=jax.ShapeDtypeStruct(green.shape...  3.27 us

profile of v8, /device:TPU:24, one launch (start us, length us, event | category | flops | bytes accessed | tf_op | source)
XLA Modules:
  0.0 61.5 jit_solution(4711282904641803025)
XLA Ops:
  0.0 0.0 copy-start.1
  0.0 0.7 %pad_add_fusion.1 = s32[32,5]{0,1:T(8,128)S(1)} fusion(s32[32,1]{0,1:T(1,128)S(1)} %iota.29, s32[32,4]{0,1:T(4,128)} %bitcast.25), kind=kLoop, calls=%fused_computation.7 | loop fusion | flops 160 | bytes 1280 | tf_op jit(solution)/shard_map/concatenate | solution.py:16
  0.8 0.1 broadcast_in_dim.6
  0.8 0.1 reshape.43
  0.9 0.2 compare_convert_fusion.1
  1.1 0.0 copy-done.1
  1.1 0.0 copy-start
  1.1 1.0 %convolution_convert_fusion = bf16[4,3,2,5,128]{4,0,3,2,1:T(4,128)(2,1)} fusion(bf16[5,128,128]{2,1,0:T(8,128)(2,1)S(1)} %compare_convert_fusion.1, bf16[3,2,128,128]{3,2,1,0:T(8,128)(2,1)S(1)} %bitcast.27, s32[128]{0:T(128)S(1)} %and_select_fusion.1), kind=kOutput, calls=%fused_computation | convolution fusion | flops 5914112 | bytes 391680 | tf_op jit(solution)/shard_map/enjrc,cp->enjpr/dot_general | solution.py:227
  2.1 55.1 %shard_map.73.sig_ref = bf16[120,128]{1,0:T(8,128)(2,1)} custom-call(bf16[3,40,128]{2,1,0:T(8,128)(2,1)} %bitcast.22, s32[16,16]{1,0:T(8,128)} %q_ref.1, f32[2,16]{1,0:T(2,128)} %c_ref.1, f32[2]{0:T(128)} %occ_ref.1, s32[2]{0:T(128)} %sh_ref.1), custom_call_target="tpu_custom_call" | custom-call | tf_op jit(solution)/shard_map/pallas_call | solution.py:148
  57.3 0.0 copy-done
  57.3 0.1 broadcast_in_dim.7
  57.4 0.1 reshape.45
  57.5 0.8 %compare_convert_fusion.maskt_ref = bf16[5,128,128]{2,1,0:T(8,128)(2,1)} fusion(s32[5,128]{1,0:T(8,128)S(1)} %bitcast.23, s32[128]{0:T(128)S(1)} %and_select_fusion), kind=kLoop, calls=%fused_computation.4 | loop fusion | flops 163840 | bytes 166912 | tf_op jit(solution)/shard_map/convert_element_type | solution.py:19
  58.3 3.3 %shard_map.74 = bf16[3,2,128,128]{3,2,1,0:T(8,128)(2,1)} custom-call(bf16[120,128]{1,0:T(8,128)(2,1)} %shard_map.73.sig_ref, bf16[3,2,128,128]{3,2,1,0:T(8,128)(2,1)} %bitcast.21, bf16[5,128,128]{2,1,0:T(8,128)(2,1)} %compare_convert_fusion.maskt_ref), custom_call_target="tpu_custom_call" | custom-call | tf_op jit(solution)/shard_map/pallas_call | solution.py:208
  (4 shorter events, 0.0 us)
Async XLA Ops:
  0.0 1.1 %copy-start.1 = (bf16[1,3,1,2,128,128]{5,4,3,2,1,0:T(8,128)(2,1)S(1)}, bf16[1,3,1,2,128,128]{5,4,3,2,1,0:T(8,128)(2,1)}, u32[]{:S(2)}) copy-start(bf16[1,3,1,2,128,128]{5,4,3,2,1,0:T(8,128)(2,1)} %param.7) | copy-start | bytes 589828
  1.1 56.2 %copy-start = (s32[1,32,4]{1,2,0:T(4,128)S(1)}, s32[1,32,4]{1,2,0:T(4,128)}, u32[]{:S(2)}) copy-start(s32[1,32,4]{1,2,0:T(4,128)} %param.9) | copy-start | bytes 1540

commit v9 on v8

--- a/solution.py
+++ b/solution.py
@@ -19,12 +19,8 @@
     return (row_pairs.T[:, :, None] == col_atom[None, None, :]).astype(jnp.bfloat16)
 
 
-def spread(width):
-    return (jnp.arange(width)[:, None] % ORB == jnp.arange(ORB)[None, :]).astype(jnp.bfloat16)
-
-
-def born_kernel(own_ref, q_ref, c_ref, occ_ref, sh_ref, out_ref, land, landf, part, relay_r, relay_l,
-                near_r, near_l, far_r, far_l, sum_r, sum_l, gsend, grecv, send, recv):
+def born_kernel(g_ref, mask_ref, q_ref, c_ref, occ_ref, sh_ref, out_ref, own_ref, land, landf, part, relay_r,
+                relay_l, near_r, near_l, far_r, far_l, sum_r, sum_l, gsend, grecv, send, recv):
     kz = lax.axis_index("kz")
     eb = lax.axis_index("energy")
     ne = lax.axis_size("energy")
@@ -47,6 +43,23 @@
         pl.semaphore_signal(barrier, 1, device_id=where(d, t), device_id_type=mesh)
     for nb in (left, right):
         pl.semaphore_signal(barrier, 1, device_id={"kz": nb}, device_id_type=mesh)
+
+    members = mask_ref.shape[0]
+    width = g_ref.shape[2]
+    line = lax.broadcasted_iota(jnp.int32, (rows, width), 0)
+    spread = lax.broadcasted_iota(jnp.int32, (rows, width), 1) & (ORB - 1)
+    for e in range(edev):
+        acc = jnp.zeros((rows, width), jnp.float32)
+        for n in range(2):
+            green = g_ref[e, n]
+            for j in range(members):
+                sel_t = jnp.where(line - (n * members + j) * ORB == spread, 1.0, 0.0).astype(green.dtype)
+                held = green * mask_ref[j]
+                acc = acc + lax.dot_general(
+                    sel_t, held, (((1,), (1,)), ((), ())), preferred_element_type=jnp.float32
+                )
+        own_ref[e] = acc.astype(own_ref.dtype)
+        landf[0, edev + e] = acc
     pl.semaphore_wait(barrier, len(peers) + 2)
 
     copies = []
@@ -57,8 +70,6 @@
         )
         c.start()
         copies.append(c)
-    for e in range(edev):
-        landf[0, edev + e] = own_ref[e].astype(jnp.float32)
     for c in copies:
         c.wait()
     keep = (jnp.where(eb > 0, 1.0, 0.0), 1.0, jnp.where(eb < ne - 1, 1.0, 0.0))
@@ -137,8 +148,10 @@
     out_ref[hi] = (part[0, hi] + near_r[...] + far_l[...]).astype(out_ref.dtype)
 
 
-def born(own, q_table, coupling, occupation, ph_shift):
-    edev, rows, lanes = own.shape
+def born(green, mask, q_table, coupling, occupation, ph_shift):
+    edev = green.shape[0]
+    lanes = green.shape[3]
+    rows = 2 * mask.shape[0] * ORB
     xs = lax.axis_size("kz") // ZHI
     total = edev * rows
     split = (total // 2 + 15) // 16 * 16
@@ -148,10 +161,11 @@
     return pl.pallas_call(
         born_kernel,
         out_shape=jax.ShapeDtypeStruct((total, lanes), jnp.bfloat16),
-        in_specs=[pl.BlockSpec(memory_space=vmem), smem, smem, smem, smem],
+        in_specs=[pl.BlockSpec(memory_space=vmem), pl.BlockSpec(memory_space=vmem), smem, smem, smem, smem],
         out_specs=pl.BlockSpec(memory_space=vmem),
         scratch_shapes=[
-            vmem((xs, 3 * edev, rows, lanes), own.dtype),
+            vmem((edev, rows, lanes), green.dtype),
+            vmem((xs, 3 * edev, rows, lanes), green.dtype),
             vmem((xs, 3 * edev, rows, lanes), f32),
             vmem((ZHI, total, lanes), f32),
             vmem((split, lanes), f32),
@@ -168,15 +182,16 @@
             pltpu.SemaphoreType.DMA((10,)),
         ],
         compiler_params=pltpu.CompilerParams(collective_id=0, has_side_effects=True),
-    )(own, q_table, coupling, occupation, ph_shift)
-
-
-def keldysh_kernel(sig_ref, green_ref, maskt_ref, out_ref):
+    )(green, mask, q_table, coupling, occupation, ph_shift)
+
+
+def keldysh_kernel(sig_ref, green_ref, mask_ref, out_ref):
     f32 = jnp.float32
     edev = green_ref.shape[0]
     rows = sig_ref.shape[0] // edev
-    members = maskt_ref.shape[0]
+    members = mask_ref.shape[0]
     width = green_ref.shape[2]
+    mask_t = [mask_ref[j].astype(f32).T for j in range(members)]
     lane = lax.broadcasted_iota(jnp.int32, (width, rows), 1)
     spread = lax.broadcasted_iota(jnp.int32, (width, rows), 0) & (ORB - 1)
 
@@ -193,7 +208,7 @@
             acc = jnp.zeros(green_ref.shape[2:], f32)
             for j in range(members):
                 tiled = jnp.dot(sel((n * members + j) * ORB), sig, preferred_element_type=f32)
-                acc = acc + tiled * maskt_ref[j].astype(f32)
+                acc = acc + tiled * mask_t[j]
             dense_t.append(acc.astype(sig.dtype))
         gr = green_ref[e, 0]
         gi = green_ref[e, 1]
@@ -203,34 +218,21 @@
         out_ref[e, 1] = (nt(pi, gr) - nt(pr, gi)).astype(out_ref.dtype)
 
 
-def keldysh(sigma, green, maskt):
+def keldysh(sigma, green, mask):
     vmem = pl.BlockSpec(memory_space=pltpu.VMEM)
     return pl.pallas_call(
         keldysh_kernel,
         out_shape=jax.ShapeDtypeStruct(green.shape, jnp.bfloat16),
         in_specs=[vmem, vmem, vmem],
         out_specs=vmem,
-    )(sigma, green, maskt)
+    )(sigma, green, mask)
 
 
 def per_device(g_less, g_ret, neighbors, ph_shift, q_table, coupling, occupation):
-    edev = g_less.shape[1]
     width = g_less.shape[4]
-    members = neighbors.shape[2] + 1
-    momenta = lax.axis_size("kz")
-    xs = momenta // ZHI
     mask = masks(neighbors, width)
-    e4 = spread(width)
-
-    green = g_less[0, :, 0]
-    held = green[:, :, None] * mask[None, None]
-    picked = jnp.einsum("enjrc,cp->enjpr", held, e4, preferred_element_type=jnp.float32)
-    picked = picked.astype(jnp.bfloat16).reshape(edev, 2 * members * ORB, width)
-    sigma = born(picked, q_table, coupling, occupation, ph_shift)
-
-    sigma, later = lax.optimization_barrier((sigma, neighbors))
-    maskt = jnp.swapaxes(masks(later, width), 1, 2)
-    result = keldysh(sigma, g_ret[0, :, 0, 0], maskt)
+    sigma = born(g_less[0, :, 0], mask, q_table, coupling, occupation, ph_shift)
+    result = keldysh(sigma, g_ret[0, :, 0, 0], mask)
     return result[None, :, None]
 
 

time: 62.2 us -> 60.8 us (0.977)
  matrix products: 1 us -> 0 us
  other arithmetic: 1.65 us -> 0.83 us
    dot_general x1 -> x0, matrix products: 1 us -> none  [per_device(): jnp.einsum('enjrc,cp->enjpr', held, e4, preferred_element_type=jnp.float32)]
    concatenate x2 -> x1, other arithmetic: 0.74 us -> 0.01 us  [masks(): pairs = jnp.concatenate([own, neighbors[0]], axis=1)]
    unnamed x4 -> x2, local copies, waits for them, and re-layouts: 0.01 us -> 0.67 us
where the time goes in v9:
time: 60.8 us; the launch traced here: 60.2 us
  Pallas kernels  58.5 us (96%)
  local copies, waits for them, and re-layouts  0.86 us (1%)
  other arithmetic  0.83 us (1%)
    pallas_call x1, Pallas kernels, born(): pl.pallas_call(born_kernel, out_shape=jax.ShapeDtypeStruct((total, lanes)...  55.2 us
    pallas_call x1, Pallas kernels, keldysh(): pl.pallas_call(keldysh_kernel, out_shape=jax.ShapeDtypeStruct(green.shape...  3.27 us

profile of v9, /device:TPU:24, one launch (start us, length us, event | category | flops | bytes accessed | tf_op | source)
XLA Modules:
  0.0 60.2 jit_solution(2005305046060423739)
XLA Ops:
  0.0 0.0 copy-start
  0.0 0.7 %copy-done = s32[1,32,4]{1,2,0:T(4,128)S(1)} copy-done((s32[1,32,4]{1,2,0:T(4,128)S(1)}, s32[1,32,4]{1,2,0:T(4,128)}, u32[]{:S(2)}) %copy-start) | copy-done | bytes 536
  0.7 0.1 broadcast_in_dim.4
  0.8 0.1 reshape.17
  0.9 0.8 %compare_convert_fusion.mask_ref = bf16[5,128,128]{2,1,0:T(8,128)(2,1)} fusion(s32[128]{0:T(128)S(1)} %and_select_fusion, s32[5,128]{1,0:T(8,128)S(1)} %bitcast.11), kind=kLoop, calls=%fused_computation | loop fusion | flops 163840 | bytes 166912 | tf_op jit(solution)/shard_map/convert_element_type | solution.py:19
  1.7 55.2 %shard_map.73.sig_ref = bf16[120,128]{1,0:T(8,128)(2,1)} custom-call(bf16[3,2,128,128]{3,2,1,0:T(8,128)(2,1)} %bitcast.9, bf16[5,128,128]{2,1,0:T(8,128)(2,1)} %compare_convert_fusion.mask_ref, s32[16,16]{1,0:T(8,128)} %q_ref.1, f32[2,16]{1,0:T(2,128)} %c_ref.1, f32[2]{0:T(128)} %occ_ref.1, s32[2]{0:T(128)} %sh_ref.1), custom_call_target="tpu_custom_call" | custom-call | tf_op jit(solution)/shard_map/pallas_call | solution.py:161
  56.9 3.3 %shard_map.74 = bf16[3,2,128,128]{3,2,1,0:T(8,128)(2,1)} custom-call(bf16[120,128]{1,0:T(8,128)(2,1)} %shard_map.73.sig_ref, bf16[3,2,128,128]{3,2,1,0:T(8,128)(2,1)} %bitcast.10, bf16[5,128,128]{2,1,0:T(8,128)(2,1)} %compare_convert_fusion.mask_ref), custom_call_target="tpu_custom_call" | custom-call | tf_op jit(solution)/shard_map/pallas_call | solution.py:223
  (3 shorter events, 0.0 us)
Async XLA Ops:
  0.0 0.7 %copy-start = (s32[1,32,4]{1,2,0:T(4,128)S(1)}, s32[1,32,4]{1,2,0:T(4,128)}, u32[]{:S(2)}) copy-start(s32[1,32,4]{1,2,0:T(4,128)} %param.9) | copy-start | bytes 1540

commit v10 on v9

--- a/solution.py
+++ b/solution.py
@@ -192,11 +192,12 @@
     members = mask_ref.shape[0]
     width = green_ref.shape[2]
     mask_t = [mask_ref[j].astype(f32).T for j in range(members)]
-    lane = lax.broadcasted_iota(jnp.int32, (width, rows), 1)
-    spread = lax.broadcasted_iota(jnp.int32, (width, rows), 0) & (ORB - 1)
-
-    def sel(base):
-        return jnp.where(lane - base == spread, 1.0, 0.0).astype(sig_ref.dtype)
+    tall = lax.broadcasted_iota(jnp.int32, (members * width, rows), 0)
+    lane = lax.broadcasted_iota(jnp.int32, (members * width, rows), 1)
+    sel = [
+        jnp.where(lane - n * members * ORB - ORB * (tall // width) == (tall & (ORB - 1)), 1.0, 0.0).astype(sig_ref.dtype)
+        for n in range(2)
+    ]
 
     def nt(a, b):
         return lax.dot_general(a, b, (((1,), (1,)), ((), ())), preferred_element_type=f32)
@@ -205,17 +206,20 @@
         sig = sig_ref[pl.ds(e * rows, rows), :]
         dense_t = []
         for n in range(2):
-            acc = jnp.zeros(green_ref.shape[2:], f32)
-            for j in range(members):
-                tiled = jnp.dot(sel((n * members + j) * ORB), sig, preferred_element_type=f32)
-                acc = acc + tiled * mask_t[j]
+            tiled = jnp.dot(sel[n], sig, preferred_element_type=f32)
+            acc = tiled[0:width] * mask_t[0]
+            for j in range(1, members):
+                acc = acc + tiled[j * width:(j + 1) * width] * mask_t[j]
             dense_t.append(acc.astype(sig.dtype))
         gr = green_ref[e, 0]
         gi = green_ref[e, 1]
-        pr = (nt(gr, dense_t[0]) - nt(gi, dense_t[1])).astype(gr.dtype)
-        pi = (nt(gr, dense_t[1]) + nt(gi, dense_t[0])).astype(gr.dtype)
-        out_ref[e, 0] = (nt(pr, gr) + nt(pi, gi)).astype(out_ref.dtype)
-        out_ref[e, 1] = (nt(pi, gr) - nt(pr, gi)).astype(out_ref.dtype)
+        blocks = nt(jnp.concatenate([gr, gi], 0), jnp.concatenate(dense_t, 0))
+        pr = (blocks[:width, :width] - blocks[width:, width:]).astype(gr.dtype)
+        pi = (blocks[:width, width:] + blocks[width:, :width]).astype(gr.dtype)
+        lhs = jnp.concatenate([jnp.concatenate([pr, pi], 1), jnp.concatenate([pi, -pr], 1)], 0)
+        both = nt(lhs, jnp.concatenate([gr, gi], 1))
+        out_ref[e, 0] = both[:width].astype(out_ref.dtype)
+        out_ref[e, 1] = both[width:].astype(out_ref.dtype)
 
 
 def keldysh(sigma, green, mask):

time: 60.8 us -> 60.7 us (level)
  no operation moved by 1% of the time
where the time goes in v10:
time: 60.7 us; the launch traced here: 60.1 us
  Pallas kernels  58.4 us (96%)
  local copies, waits for them, and re-layouts  0.86 us (1%)
  other arithmetic  0.83 us (1%)
    pallas_call x1, Pallas kernels, born(): pl.pallas_call(born_kernel, out_shape=jax.ShapeDtypeStruct((total, lanes)...  55.2 us
    pallas_call x1, Pallas kernels, keldysh(): pl.pallas_call(keldysh_kernel, out_shape=jax.ShapeDtypeStruct(green.shape...  3.21 us

profile of v10, /device:TPU:24, one launch (start us, length us, event | category | flops | bytes accessed | tf_op | source)
XLA Modules:
  0.0 60.1 jit_solution(10759721642182256244)
XLA Ops:
  0.0 0.0 copy-start
  0.0 0.7 %copy-done = s32[1,32,4]{1,2,0:T(4,128)S(1)} copy-done((s32[1,32,4]{1,2,0:T(4,128)S(1)}, s32[1,32,4]{1,2,0:T(4,128)}, u32[]{:S(2)}) %copy-start) | copy-done | bytes 536
  0.7 0.1 broadcast_in_dim.4
  0.8 0.1 reshape.17
  0.9 0.8 %compare_convert_fusion.mask_ref = bf16[5,128,128]{2,1,0:T(8,128)(2,1)} fusion(s32[128]{0:T(128)S(1)} %and_select_fusion, s32[5,128]{1,0:T(8,128)S(1)} %bitcast.11), kind=kLoop, calls=%fused_computation | loop fusion | flops 163840 | bytes 166912 | tf_op jit(solution)/shard_map/convert_element_type | solution.py:19
  1.7 55.2 %shard_map.73.sig_ref = bf16[120,128]{1,0:T(8,128)(2,1)} custom-call(bf16[3,2,128,128]{3,2,1,0:T(8,128)(2,1)} %bitcast.9, bf16[5,128,128]{2,1,0:T(8,128)(2,1)} %compare_convert_fusion.mask_ref, s32[16,16]{1,0:T(8,128)} %q_ref.1, f32[2,16]{1,0:T(2,128)} %c_ref.1, f32[2]{0:T(128)} %occ_ref.1, s32[2]{0:T(128)} %sh_ref.1), custom_call_target="tpu_custom_call" | custom-call | tf_op jit(solution)/shard_map/pallas_call | solution.py:161
  56.9 3.2 %shard_map.74 = bf16[3,2,128,128]{3,2,1,0:T(8,128)(2,1)} custom-call(bf16[120,128]{1,0:T(8,128)(2,1)} %shard_map.73.sig_ref, bf16[3,2,128,128]{3,2,1,0:T(8,128)(2,1)} %bitcast.10, bf16[5,128,128]{2,1,0:T(8,128)(2,1)} %compare_convert_fusion.mask_ref), custom_call_target="tpu_custom_call" | custom-call | tf_op jit(solution)/shard_map/pallas_call | solution.py:227
  (3 shorter events, 0.0 us)
Async XLA Ops:
  0.0 0.7 %copy-start = (s32[1,32,4]{1,2,0:T(4,128)S(1)}, s32[1,32,4]{1,2,0:T(4,128)}, u32[]{:S(2)}) copy-start(s32[1,32,4]{1,2,0:T(4,128)} %param.9) | copy-start | bytes 1540

commit v11 on v10

--- a/solution.py
+++ b/solution.py
@@ -19,8 +19,8 @@
     return (row_pairs.T[:, :, None] == col_atom[None, None, :]).astype(jnp.bfloat16)
 
 
-def born_kernel(g_ref, mask_ref, q_ref, c_ref, occ_ref, sh_ref, out_ref, own_ref, land, landf, part, relay_r,
-                relay_l, near_r, near_l, far_r, far_l, sum_r, sum_l, gsend, grecv, send, recv):
+def born_kernel(g_hbm, mask_ref, q_ref, c_ref, occ_ref, sh_ref, out_ref, g_ref, g_sem, own_ref, land, landf, part,
+                relay_r, relay_l, near_r, near_l, far_r, far_l, sum_r, sum_l, gsend, grecv, send, recv):
     kz = lax.axis_index("kz")
     eb = lax.axis_index("energy")
     ne = lax.axis_size("energy")
@@ -38,11 +38,14 @@
     def where(d, t):
         return {"kz": ((x + d) % xs) * ZHI + h, "energy": (eb + t + ne) % ne}
 
+    fetch = pltpu.make_async_copy(g_hbm, g_ref, g_sem)
+    fetch.start()
     barrier = pltpu.get_barrier_semaphore()
     for d, t in peers:
         pl.semaphore_signal(barrier, 1, device_id=where(d, t), device_id_type=mesh)
     for nb in (left, right):
         pl.semaphore_signal(barrier, 1, device_id={"kz": nb}, device_id_type=mesh)
+    fetch.wait()
 
     members = mask_ref.shape[0]
     width = g_ref.shape[2]
@@ -161,9 +164,11 @@
     return pl.pallas_call(
         born_kernel,
         out_shape=jax.ShapeDtypeStruct((total, lanes), jnp.bfloat16),
-        in_specs=[pl.BlockSpec(memory_space=vmem), pl.BlockSpec(memory_space=vmem), smem, smem, smem, smem],
+        in_specs=[pl.BlockSpec(memory_space=pl.ANY), pl.BlockSpec(memory_space=vmem), smem, smem, smem, smem],
         out_specs=pl.BlockSpec(memory_space=vmem),
         scratch_shapes=[
+            vmem(green.shape, green.dtype),
+            pltpu.SemaphoreType.DMA(()),
             vmem((edev, rows, lanes), green.dtype),
             vmem((xs, 3 * edev, rows, lanes), green.dtype),
             vmem((xs, 3 * edev, rows, lanes), f32),

time: 60.7 us -> 60.7 us (level)
  no operation moved by 1% of the time
where the time goes in v11:
time: 60.7 us; the launch traced here: 60.1 us
  Pallas kernels  58.4 us (96%)
  local copies, waits for them, and re-layouts  0.86 us (1%)
  other arithmetic  0.83 us (1%)
    pallas_call x1, Pallas kernels, born(): pl.pallas_call(born_kernel, out_shape=jax.ShapeDtypeStruct((total, lanes)...  55.2 us
    pallas_call x1, Pallas kernels, keldysh(): pl.pallas_call(keldysh_kernel, out_shape=jax.ShapeDtypeStruct(green.shape...  3.21 us

profile of v11, /device:TPU:24, one launch (start us, length us, event | category | flops | bytes accessed | tf_op | source)
XLA Modules:
  0.0 60.1 jit_solution(8626786682448114417)
XLA Ops:
  0.0 0.0 copy-start
  0.0 0.7 %copy-done = s32[1,32,4]{1,2,0:T(4,128)S(1)} copy-done((s32[1,32,4]{1,2,0:T(4,128)S(1)}, s32[1,32,4]{1,2,0:T(4,128)}, u32[]{:S(2)}) %copy-start) | copy-done | bytes 536
  0.7 0.1 broadcast_in_dim.4
  0.8 0.1 reshape.17
  0.9 0.8 %compare_convert_fusion.mask_ref = bf16[5,128,128]{2,1,0:T(8,128)(2,1)} fusion(s32[128]{0:T(128)S(1)} %and_select_fusion, s32[5,128]{1,0:T(8,128)S(1)} %bitcast.11), kind=kLoop, calls=%fused_computation | loop fusion | flops 163840 | bytes 166912 | tf_op jit(solution)/shard_map/convert_element_type | solution.py:19
  1.7 55.2 %shard_map.73.sig_ref = bf16[120,128]{1,0:T(8,128)(2,1)} custom-call(bf16[3,2,128,128]{3,2,1,0:T(8,128)(2,1)} %bitcast.9, bf16[5,128,128]{2,1,0:T(8,128)(2,1)} %compare_convert_fusion.mask_ref, s32[16,16]{1,0:T(8,128)} %q_ref.1, f32[2,16]{1,0:T(2,128)} %c_ref.1, f32[2]{0:T(128)} %occ_ref.1, s32[2]{0:T(128)} %sh_ref.1), custom_call_target="tpu_custom_call" | custom-call | tf_op jit(solution)/shard_map/pallas_call | solution.py:164
  56.9 3.2 %shard_map.74 = bf16[3,2,128,128]{3,2,1,0:T(8,128)(2,1)} custom-call(bf16[120,128]{1,0:T(8,128)(2,1)} %shard_map.73.sig_ref, bf16[3,2,128,128]{3,2,1,0:T(8,128)(2,1)} %bitcast.10, bf16[5,128,128]{2,1,0:T(8,128)(2,1)} %compare_convert_fusion.mask_ref), custom_call_target="tpu_custom_call" | custom-call | tf_op jit(solution)/shard_map/pallas_call | solution.py:232
  (3 shorter events, 0.0 us)
Async XLA Ops:
  0.0 0.7 %copy-start = (s32[1,32,4]{1,2,0:T(4,128)S(1)}, s32[1,32,4]{1,2,0:T(4,128)}, u32[]{:S(2)}) copy-start(s32[1,32,4]{1,2,0:T(4,128)} %param.9) | copy-start | bytes 1540

commit v12 on v10

--- a/solution.py
+++ b/solution.py
@@ -10,16 +10,7 @@
 ZHI = 4
 
 
-def masks(neighbors, width):
-    atoms = width // ORB
-    own = jnp.arange(atoms, dtype=jnp.int32)[:, None]
-    pairs = jnp.concatenate([own, neighbors[0]], axis=1)
-    row_pairs = jnp.repeat(pairs, ORB, axis=0)
-    col_atom = jnp.arange(width, dtype=jnp.int32) // ORB
-    return (row_pairs.T[:, :, None] == col_atom[None, None, :]).astype(jnp.bfloat16)
-
-
-def born_kernel(g_ref, mask_ref, q_ref, c_ref, occ_ref, sh_ref, out_ref, own_ref, land, landf, part, relay_r,
+def born_kernel(g_ref, nb_ref, q_ref, c_ref, occ_ref, sh_ref, out_ref, mask_ref, own_ref, land, landf, part, relay_r,
                 relay_l, near_r, near_l, far_r, far_l, sum_r, sum_l, gsend, grecv, send, recv):
     kz = lax.axis_index("kz")
     eb = lax.axis_index("energy")
@@ -44,8 +35,17 @@
     for nb in (left, right):
         pl.semaphore_signal(barrier, 1, device_id={"kz": nb}, device_id_type=mesh)
 
+    width = g_ref.shape[2]
+    row_atom = lax.broadcasted_iota(jnp.int32, (width, width), 0) // ORB
+    col_atom = lax.broadcasted_iota(jnp.int32, (width, width), 1) // ORB
+    mask_ref[0] = jnp.where(row_atom == col_atom, 1.0, 0.0).astype(mask_ref.dtype)
+    for j in range(1, mask_ref.shape[0]):
+        member = jnp.zeros((width, width), jnp.int32)
+        for a in range(width // ORB):
+            member = jnp.where(row_atom == a, nb_ref[a, j - 1], member)
+        mask_ref[j] = jnp.where(member == col_atom, 1.0, 0.0).astype(mask_ref.dtype)
+
     members = mask_ref.shape[0]
-    width = g_ref.shape[2]
     line = lax.broadcasted_iota(jnp.int32, (rows, width), 0)
     spread = lax.broadcasted_iota(jnp.int32, (rows, width), 1) & (ORB - 1)
     for e in range(edev):
@@ -148,10 +148,11 @@
     out_ref[hi] = (part[0, hi] + near_r[...] + far_l[...]).astype(out_ref.dtype)
 
 
-def born(green, mask, q_table, coupling, occupation, ph_shift):
+def born(green, neighbors, q_table, coupling, occupation, ph_shift):
     edev = green.shape[0]
     lanes = green.shape[3]
-    rows = 2 * mask.shape[0] * ORB
+    members = neighbors.shape[1] + 1
+    rows = 2 * members * ORB
     xs = lax.axis_size("kz") // ZHI
     total = edev * rows
     split = (total // 2 + 15) // 16 * 16
@@ -160,9 +161,12 @@
     f32 = jnp.float32
     return pl.pallas_call(
         born_kernel,
-        out_shape=jax.ShapeDtypeStruct((total, lanes), jnp.bfloat16),
-        in_specs=[pl.BlockSpec(memory_space=vmem), pl.BlockSpec(memory_space=vmem), smem, smem, smem, smem],
-        out_specs=pl.BlockSpec(memory_space=vmem),
+        out_shape=(
+            jax.ShapeDtypeStruct((total, lanes), jnp.bfloat16),
+            jax.ShapeDtypeStruct((members, lanes, lanes), jnp.bfloat16),
+        ),
+        in_specs=[pl.BlockSpec(memory_space=vmem), smem, smem, smem, smem, smem],
+        out_specs=(pl.BlockSpec(memory_space=vmem), pl.BlockSpec(memory_space=vmem)),
         scratch_shapes=[
             vmem((edev, rows, lanes), green.dtype),
             vmem((xs, 3 * edev, rows, lanes), green.dtype),
@@ -182,7 +186,7 @@
             pltpu.SemaphoreType.DMA((10,)),
         ],
         compiler_params=pltpu.CompilerParams(collective_id=0, has_side_effects=True),
-    )(green, mask, q_table, coupling, occupation, ph_shift)
+    )(green, neighbors, q_table, coupling, occupation, ph_shift)
 
 
 def keldysh_kernel(sig_ref, green_ref, mask_ref, out_ref):
@@ -233,9 +237,7 @@
 
 
 def per_device(g_less, g_ret, neighbors, ph_shift, q_table, coupling, occupation):
-    width = g_less.shape[4]
-    mask = masks(neighbors, width)
-    sigma = born(g_less[0, :, 0], mask, q_table, coupling, occupation, ph_shift)
+    sigma, mask = born(g_less[0, :, 0], neighbors[0], q_table, coupling, occupation, ph_shift)
     result = keldysh(sigma, g_ret[0, :, 0, 0], mask)
     return result[None, :, None]
 

time: 60.7 us -> 60.7 us (level)
  other arithmetic: 0.83 us -> 0 us
    convert_element_type x1 -> x0, other arithmetic: 0.82 us -> none  [masks(): (row_pairs.T[:, :, None] == col_atom[None, None, :]).astype(jnp.bfloat16)]
    squeeze x0 -> x1, local copies, waits for them, and re-layouts: none -> 0.69 us  [per_device(): neighbors[0]]
where the time goes in v12:
time: 60.7 us; the launch traced here: 60.1 us
  Pallas kernels  58.7 us (97%)
  local copies, waits for them, and re-layouts  1.37 us (2%)
    pallas_call x1, Pallas kernels, born(): pl.pallas_call(born_kernel, out_shape=(jax.ShapeDtypeStruct((total, lanes...  55.5 us
    pallas_call x1, Pallas kernels, keldysh(): pl.pallas_call(keldysh_kernel, out_shape=jax.ShapeDtypeStruct(green.shape...  3.21 us

profile of v12, /device:TPU:24, one launch (start us, length us, event | category | flops | bytes accessed | tf_op | source)
XLA Modules:
  0.0 60.1 jit_solution(6703319946863885819)
XLA Ops:
  0.0 0.0 copy-start
  0.0 0.7 %copy-done = s32[1,32,4]{1,2,0:T(4,128)S(1)} copy-done((s32[1,32,4]{1,2,0:T(4,128)S(1)}, s32[1,32,4]{1,2,0:T(4,128)}, u32[]{:S(2)}) %copy-start) | copy-done | bytes 536
  0.7 0.7 %copy.8.nb_ref = s32[32,4]{1,0:T(8,128)} copy(s32[32,4]{0,1:T(4,128)S(1)} %bitcast.8) | data formatting | bytes 1024 | tf_op jit(solution)/shard_map/squeeze | solution.py:240
  1.4 55.5 %shard_map.73 = (bf16[120,128]{1,0:T(8,128)(2,1)}, bf16[5,128,128]{2,1,0:T(8,128)(2,1)}) custom-call(bf16[3,2,128,128]{3,2,1,0:T(8,128)(2,1)} %bitcast.6, s32[32,4]{1,0:T(8,128)} %copy.8.nb_ref, s32[16,16]{1,0:T(8,128)} %q_ref.1, f32[2,16]{1,0:T(2,128)} %c_ref.1, f32[2]{0:T(128)} %occ_ref.1, s32[2]{0:T(128)} %sh_ref.1), custom_call_target="tpu_custom_call" | custom-call | tf_op jit(solution)/shard_map/pallas_call | solution.py:162
  56.9 3.2 %shard_map.74 = bf16[3,2,128,128]{3,2,1,0:T(8,128)(2,1)} custom-call(bf16[120,128]{1,0:T(8,128)(2,1)} %get-tuple-element.7.sig_ref, bf16[3,2,128,128]{3,2,1,0:T(8,128)(2,1)} %bitcast.7, bf16[5,128,128]{2,1,0:T(8,128)(2,1)} %get-tuple-element.8.mask_ref), custom_call_target="tpu_custom_call" | custom-call | tf_op jit(solution)/shard_map/pallas_call | solution.py:231
Async XLA Ops:
  0.0 0.7 %copy-start = (s32[1,32,4]{1,2,0:T(4,128)S(1)}, s32[1,32,4]{1,2,0:T(4,128)}, u32[]{:S(2)}) copy-start(s32[1,32,4]{1,2,0:T(4,128)} %param.9) | copy-start | bytes 1540

commit v13 on v12

--- a/solution.py
+++ b/solution.py
@@ -70,15 +70,12 @@
         )
         c.start()
         copies.append(c)
-    for c in copies:
+    keep = (jnp.where(eb > 0, 1.0, 0.0), 1.0, jnp.where(eb < ne - 1, 1.0, 0.0))
+    for c, (d, t) in zip(copies, peers):
         c.wait()
-    keep = (jnp.where(eb > 0, 1.0, 0.0), 1.0, jnp.where(eb < ne - 1, 1.0, 0.0))
-    for d in range(xs):
-        for side in range(3):
-            if (d, side) == (0, 1):
-                continue
-            for e in range(edev):
-                landf[d, side * edev + e] = land[d, side * edev + e].astype(jnp.float32) * keep[side]
+        side = 1 - t
+        for e in range(edev):
+            landf[d, side * edev + e] = land[d, side * edev + e].astype(jnp.float32) * keep[side]
 
     shifts = [sh_ref[m] for m in range(NMODE)]
 

time: 60.7 us -> 60.6 us (level)
  no operation moved by 1% of the time
where the time goes in v13:
time: 60.6 us; the launch traced here: 60.1 us
  Pallas kernels  58.7 us (97%)
  local copies, waits for them, and re-layouts  1.37 us (2%)
    pallas_call x1, Pallas kernels, born(): pl.pallas_call(born_kernel, out_shape=(jax.ShapeDtypeStruct((total, lanes...  55.5 us
    pallas_call x1, Pallas kernels, keldysh(): pl.pallas_call(keldysh_kernel, out_shape=jax.ShapeDtypeStruct(green.shape...  3.21 us

profile of v13, /device:TPU:24, one launch (start us, length us, event | category | flops | bytes accessed | tf_op | source)
XLA Modules:
  0.0 60.1 jit_solution(6057299460477079521)
XLA Ops:
  0.0 0.0 copy-start
  0.0 0.7 %copy-done = s32[1,32,4]{1,2,0:T(4,128)S(1)} copy-done((s32[1,32,4]{1,2,0:T(4,128)S(1)}, s32[1,32,4]{1,2,0:T(4,128)}, u32[]{:S(2)}) %copy-start) | copy-done | bytes 536
  0.7 0.7 %copy.8.nb_ref = s32[32,4]{1,0:T(8,128)} copy(s32[32,4]{0,1:T(4,128)S(1)} %bitcast.8) | data formatting | bytes 1024 | tf_op jit(solution)/shard_map/squeeze | solution.py:237
  1.4 55.5 %shard_map.73 = (bf16[120,128]{1,0:T(8,128)(2,1)}, bf16[5,128,128]{2,1,0:T(8,128)(2,1)}) custom-call(bf16[3,2,128,128]{3,2,1,0:T(8,128)(2,1)} %bitcast.6, s32[32,4]{1,0:T(8,128)} %copy.8.nb_ref, s32[16,16]{1,0:T(8,128)} %q_ref.1, f32[2,16]{1,0:T(2,128)} %c_ref.1, f32[2]{0:T(128)} %occ_ref.1, s32[2]{0:T(128)} %sh_ref.1), custom_call_target="tpu_custom_call" | custom-call | tf_op jit(solution)/shard_map/pallas_call | solution.py:159
  56.8 3.2 %shard_map.74 = bf16[3,2,128,128]{3,2,1,0:T(8,128)(2,1)} custom-call(bf16[120,128]{1,0:T(8,128)(2,1)} %get-tuple-element.7.sig_ref, bf16[3,2,128,128]{3,2,1,0:T(8,128)(2,1)} %bitcast.7, bf16[5,128,128]{2,1,0:T(8,128)(2,1)} %get-tuple-element.8.mask_ref), custom_call_target="tpu_custom_call" | custom-call | tf_op jit(solution)/shard_map/pallas_call | solution.py:228
Async XLA Ops:
  0.0 0.7 %copy-start = (s32[1,32,4]{1,2,0:T(4,128)S(1)}, s32[1,32,4]{1,2,0:T(4,128)}, u32[]{:S(2)}) copy-start(s32[1,32,4]{1,2,0:T(4,128)} %param.9) | copy-start | bytes 1540

commit v14 on v12

--- a/solution.py
+++ b/solution.py
@@ -10,7 +10,7 @@
 ZHI = 4
 
 
-def born_kernel(g_ref, nb_ref, q_ref, c_ref, occ_ref, sh_ref, out_ref, mask_ref, own_ref, land, landf, part, relay_r,
+def born_kernel(g_ref, nb_ref, q_ref, c_ref, occ_ref, sh_ref, ret_ref, result_ref, out_ref, mask_ref, own_ref, land, landf, part, relay_r,
                 relay_l, near_r, near_l, far_r, far_l, sum_r, sum_l, gsend, grecv, send, recv):
     kz = lax.axis_index("kz")
     eb = lax.axis_index("energy")
@@ -146,9 +146,10 @@
     hi = pl.ds(split, total - split)
     out_ref[lo] = (part[0, lo] + near_l[...] + far_r[...]).astype(out_ref.dtype)
     out_ref[hi] = (part[0, hi] + near_r[...] + far_l[...]).astype(out_ref.dtype)
-
-
-def born(green, neighbors, q_table, coupling, occupation, ph_shift):
+    keldysh_kernel(out_ref, ret_ref, mask_ref, result_ref)
+
+
+def born(green, neighbors, q_table, coupling, occupation, ph_shift, retarded):
     edev = green.shape[0]
     lanes = green.shape[3]
     members = neighbors.shape[1] + 1
@@ -161,13 +162,12 @@
     f32 = jnp.float32
     return pl.pallas_call(
         born_kernel,
-        out_shape=(
-            jax.ShapeDtypeStruct((total, lanes), jnp.bfloat16),
-            jax.ShapeDtypeStruct((members, lanes, lanes), jnp.bfloat16),
-        ),
-        in_specs=[pl.BlockSpec(memory_space=vmem), smem, smem, smem, smem, smem],
-        out_specs=(pl.BlockSpec(memory_space=vmem), pl.BlockSpec(memory_space=vmem)),
+        out_shape=jax.ShapeDtypeStruct(retarded.shape, jnp.bfloat16),
+        in_specs=[pl.BlockSpec(memory_space=vmem), smem, smem, smem, smem, smem, pl.BlockSpec(memory_space=vmem)],
+        out_specs=pl.BlockSpec(memory_space=vmem),
         scratch_shapes=[
+            vmem((total, lanes), jnp.bfloat16),
+            vmem((members, lanes, lanes), jnp.bfloat16),
             vmem((edev, rows, lanes), green.dtype),
             vmem((xs, 3 * edev, rows, lanes), green.dtype),
             vmem((xs, 3 * edev, rows, lanes), f32),
@@ -186,7 +186,7 @@
             pltpu.SemaphoreType.DMA((10,)),
         ],
         compiler_params=pltpu.CompilerParams(collective_id=0, has_side_effects=True),
-    )(green, neighbors, q_table, coupling, occupation, ph_shift)
+    )(green, neighbors, q_table, coupling, occupation, ph_shift, retarded)
 
 
 def keldysh_kernel(sig_ref, green_ref, mask_ref, out_ref):
@@ -237,8 +237,7 @@
 
 
 def per_device(g_less, g_ret, neighbors, ph_shift, q_table, coupling, occupation):
-    sigma, mask = born(g_less[0, :, 0], neighbors[0], q_table, coupling, occupation, ph_shift)
-    result = keldysh(sigma, g_ret[0, :, 0, 0], mask)
+    result = born(g_less[0, :, 0], neighbors[0], q_table, coupling, occupation, ph_shift, g_ret[0, :, 0, 0])
     return result[None, :, None]
 
 

time: 60.7 us -> 60.7 us (level)
  Pallas kernels: 58.7 us -> 57 us
  local copies, waits for them, and re-layouts: 1.37 us -> 2.99 us
    pallas_call x2 -> x1, Pallas kernels: 58.7 us -> 57 us  [born(): pl.pallas_call(born_kernel, out_shape=jax.ShapeDtypeStruct(retarded.shape...]
    unnamed x2 -> x3, local copies, waits for them, and re-layouts: 0.68 us -> 2.3 us
where the time goes in v14:
time: 60.7 us; the launch traced here: 60 us
  Pallas kernels  57 us (94%)
  local copies, waits for them, and re-layouts  2.99 us (5%)
    pallas_call x1, Pallas kernels, born(): pl.pallas_call(born_kernel, out_shape=jax.ShapeDtypeStruct(retarded.shape...  57 us
    unnamed x3, local copies, waits for them, and re-layouts  2.3 us

profile of v14, /device:TPU:24, one launch (start us, length us, event | category | flops | bytes accessed | tf_op | source)
XLA Modules:
  0.0 60.0 jit_solution(4841244124051291465)
XLA Ops:
  0.0 0.0 copy-start
  0.0 0.7 %copy-done = s32[1,32,4]{1,2,0:T(4,128)S(1)} copy-done((s32[1,32,4]{1,2,0:T(4,128)S(1)}, s32[1,32,4]{1,2,0:T(4,128)}, u32[]{:S(2)}) %copy-start) | copy-done | bytes 536
  0.7 0.7 %copy.8.nb_ref = s32[32,4]{1,0:T(8,128)} copy(s32[32,4]{0,1:T(4,128)S(1)} %bitcast.9) | data formatting | bytes 1024 | tf_op jit(solution)/shard_map/squeeze | solution.py:240
  1.4 57.0 %shard_map.73 = bf16[3,2,128,128]{3,2,1,0:T(8,128)(2,1)} custom-call(bf16[3,2,128,128]{3,2,1,0:T(8,128)(2,1)} %bitcast.7, s32[32,4]{1,0:T(8,128)} %copy.8.nb_ref, s32[16,16]{1,0:T(8,128)} %q_ref.1, f32[2,16]{1,0:T(2,128)} %c_ref.1, f32[2]{0:T(128)} %occ_ref.1, s32[2]{0:T(128)} %sh_ref.1, bf16[3,2,128,128]{3,2,1,0:T(8,128)(2,1)} %bitcast.8), custom_call_target="tpu_custom_call" | custom-call | tf_op jit(solution)/shard_map/pallas_call | solution.py:163
  58.4 1.6 %copy.11 = bf16[1,3,1,2,128,128]{5,4,3,2,1,0:T(8,128)(2,1)} copy(bf16[1,3,1,2,128,128]{5,4,3,2,1,0:T(8,128)(2,1)} %bitcast.6) | data formatting | bytes 393216
Async XLA Ops:
  0.0 0.7 %copy-start = (s32[1,32,4]{1,2,0:T(4,128)S(1)}, s32[1,32,4]{1,2,0:T(4,128)}, u32[]{:S(2)}) copy-start(s32[1,32,4]{1,2,0:T(4,128)} %param.9) | copy-start | bytes 1540
